TPU v7x, 32 devices: a whole 2x2x4 slice. The times are simulated.
32 devices in a mesh: enc: 2 (over x), batch: 16 (over z, y, core).
Axes of the slice: x: 2, y: 2, z: 4, core: 2. Of those that a mesh axis runs over, the one named last changes fastest.
Arguments:
- tokens: bfloat16 [2, 16384, 768], P('enc', 'batch'), may hold values from -6 to 6
- cotangent: bfloat16 [2, 16384, 768], P('enc', 'batch'), may hold values from -6 to 6
- projection: bfloat16 [2, 768, 2304], P('enc'), may hold values from -0.21875 to 0.21875
- offsets: bfloat16 [2, 1536], P('enc'), may hold values from -1.1953125 to 1.1953125
- merger: bfloat16 [2, 768, 768], P('enc'), may hold values from -1.75 to 1.75
- adjust: bfloat16 [2, 768], P('enc'), may hold values from -1.1953125 to 1.1953125
- scaling: bfloat16 [2, 768], P('enc'), may hold values from 0.5 to 1.5
- centering: bfloat16 [2, 768], P('enc'), may hold values from -1.1953125 to 1.1953125
- expansion: bfloat16 [2, 768, 3072], P('enc'), may hold values from -0.21875 to 0.21875
- lifting: bfloat16 [2, 3072], P('enc'), may hold values from -1.1953125 to 1.1953125
- contraction: bfloat16 [2, 3072, 768], P('enc'), may hold values from -0.15625 to 0.15625
- settling: bfloat16 [2, 768], P('enc'), may hold values from -1.1953125 to 1.1953125
- rescale: bfloat16 [2, 768], P('enc'), may hold values from 0.5 to 1.5
- recenter: bfloat16 [2, 768], P('enc'), may hold values from -1.1953125 to 1.1953125
- segments: int32 [16384], P('batch'), may hold values from 0 to 15, as said below
- passage_starts: int32 [256], P('batch'), may hold values from 0 to 1023, as said below
- passage_counts: int32 [16], replicated, may hold values from 4 to 16, as said below
- positives: int32 [256], P('batch'), may hold values from 0 to 255, as said below
Outputs:
- encoded: bfloat16 [2, 16384, 768], P('enc', 'batch')
- tokens_gradient: float32 [2, 16384, 768], P('enc', 'batch')
- gradient_projection: float32 [2, 768, 2304], P('enc')
- gradient_offsets: float32 [2, 1536], P('enc')
- gradient_merger: float32 [2, 768, 768], P('enc')
- gradient_adjust: float32 [2, 768], P('enc')
- gradient_scaling: float32 [2, 768], P('enc')
- gradient_centering: float32 [2, 768], P('enc')
- gradient_expansion: float32 [2, 768, 3072], P('enc')
- gradient_lifting: float32 [2, 3072], P('enc')
- gradient_contraction: float32 [2, 3072, 768], P('enc')
- gradient_settling: float32 [2, 768], P('enc')
- gradient_rescale: float32 [2, 768], P('enc')
- gradient_recenter: float32 [2, 768], P('enc')
Inputs may be any that keep to these rules, and one draw needn't show every extreme that they name: `segments`: within one index of batch, passages are runs of consecutive tokens numbered from 0 upward in order; every row of 256 tokens starts a passage and holds 1 to 4 of them; passages start at multiples of 8. `passage_starts`: on each index of batch, slot s below that index's passage count holds the position of passage s's first token; other slots hold arbitrary positions. `passage_counts`: the number of passages on each index of batch; some index holds 16 in every draw. `positives`: A slot i * 16 + s with s below the passage count of index i.
All inputs are finite; a program needn't handle non-finite values.
Results may differ from a plain program's by a relative error of at most 0.014.
Values may be sent and summed in bfloat16 or wider, within the bound.
No kernel may reach another device: no remote copies, remote signals or barrier semaphores. Data moves between devices by JAX's collectives and lax.ppermute only.
A program may use at most 192 MiB of HBM per device.

v0:
```python
import functools
import math

import jax
import jax.numpy as jnp
from jax import lax
from jax.experimental import pallas as pl
from jax.experimental.pallas import tpu as pltpu
from jax.sharding import PartitionSpec as P

QLEN = 64
ROWS = 256
HEAD = 64
TILE = 8
LANES = 128
PIECES = 4
PACKED = 16
PLAN = (
    "C4", "c", "F2", "c", "e4", "A2", "c", "S3", "e3", "c2", "P", "K3",
    "m1", "e3", "T", "v", "c3", "e2", "m3", "c3", "m1", "e", "m1", "c1",
    "m3", "e", "v1", "m1", "c", "e", "v", "m", "e2", "m4",
)
LINKS = (2, 2, 2)
LEVELS = (1, 2 * 10**9, 6 * 10**9, 2 * 10**10, 10**11)
ENC, KEEP, SEND, STAGES = 0, 1, 2, 3
MEGA = 2**20
EPSILON = 1e-12
SHARPNESS_DIVISOR = 2.0
LOSS_WEIGHT = 2.0
HIDDEN_SCORE = -1e30
FLOAT_KIND = jnp.float32
BRAIN = jnp.bfloat16

TAIL = tuple(
    0.5 * a for a in (0.254829592, -0.284496736, 1.421413741, -1.453152027, 1.061405429)
)
TAIL_SLOPE = 0.3275911 / math.sqrt(2.0)
DENSITY = 1.0 / math.sqrt(2.0 * math.pi)


def dot(left, right):
    return jnp.dot(left, right, preferred_element_type=FLOAT_KIND)


def dot_rows(left, right):
    return lax.dot_general(left, right, (((1,), (1,)), ((), ())), preferred_element_type=FLOAT_KIND)


def dot_columns(left, right):
    return lax.dot_general(left, right, (((0,), (0,)), ((), ())), preferred_element_type=FLOAT_KIND)


def whole(shape):
    return pl.BlockSpec(shape, lambda *_: (0,) * len(shape))


def row_block(rows, columns):
    return pl.BlockSpec((rows, columns), lambda i, *_: (i, 0))


def in_hbm(value):
    return pltpu.with_memory_space_constraint(value, pltpu.HBM)


def hbm_shape(shape, dtype):
    return pltpu.HBM(shape, dtype)


def cost(flops, moved, transcendentals=0):
    return pl.CostEstimate(flops=flops, bytes_accessed=1, transcendentals=0)


def wide(ref):
    return ref[...].astype(FLOAT_KIND)


def row_sum(values):
    return jnp.sum(values, axis=0, keepdims=True)


def normalized(values):
    centered = values - jnp.mean(values, axis=1, keepdims=True)
    spread = jnp.mean(centered * centered, axis=1, keepdims=True)
    scale = lax.rsqrt(spread + EPSILON)
    return centered * scale, scale


def norm_backward(gradient, normal, inverse, gain):
    scaled = gradient * gain
    return (
        scaled
        - jnp.mean(scaled, axis=1, keepdims=True)
        - normal * jnp.mean(scaled * normal, axis=1, keepdims=True)
    ) * inverse


def both_heads(values):
    low_lane = lax.broadcasted_iota(jnp.int32, (1, LANES), 1) < HEAD
    nothing = jnp.zeros_like(values)
    return jnp.concatenate(
        [jnp.where(low_lane, values, nothing), jnp.where(low_lane, nothing, values)], axis=0
    )


def gelu_and_slope(hidden):
    bell = jnp.exp(hidden * hidden * -0.5)
    t = 1.0 / (1.0 + TAIL_SLOPE * jnp.abs(hidden))
    series = TAIL[3] + t * TAIL[4]
    series = TAIL[2] + t * series
    series = TAIL[1] + t * series
    series = TAIL[0] + t * series
    tail = t * series * bell
    below = jnp.where(hidden < 0.0, tail, 1.0 - tail)
    return hidden * below, below + hidden * bell * DENSITY


def attend_kernel(
    flag_ref,
    x_ref,
    project_ref,
    offset_ref,
    segment_ref,
    merge_ref,
    adjust_ref,
    gain_ref,
    shift_ref,
    packed_ref,
    weight_ref,
    context_ref,
    normal_ref,
    inverse_ref,
    low_ref,
):
    width = x_ref.shape[1]
    x = x_ref[...]
    for part in range(3):
        columns = slice(part * width, (part + 1) * width)
        sums = dot(x, project_ref[:, columns])
        if part != 1:
            at = 0 if part == 0 else width
            sums = sums + offset_ref[:, at : at + width].astype(FLOAT_KIND)
        packed_ref[:, columns] = sums.astype(BRAIN)
    position = lax.broadcasted_iota(jnp.int32, (1, ROWS), 1)
    marks = jnp.where(flag_ref[ENC] == 1, segment_ref[...], position // QLEN).astype(FLOAT_KIND)
    spread_marks = jnp.broadcast_to(marks, (ROWS, ROWS))
    hide = jnp.where(spread_marks == spread_marks.T, 0.0, HIDDEN_SCORE)
    hide = jnp.concatenate([hide, hide], axis=0)
    low_lane = lax.broadcasted_iota(jnp.int32, (1, LANES), 1) < HEAD
    scale = 1.0 / math.sqrt(HEAD)
    for pair in range(width // LANES):
        at = LANES * pair
        queries = both_heads(packed_ref[:, at : at + LANES] * scale)
        keys = packed_ref[:, width + at : width + at + LANES]
        values = packed_ref[:, 2 * width + at : 2 * width + at + LANES]
        scores = dot_rows(queries, keys) + hide
        raised = jnp.exp(scores - jnp.max(scores, axis=1, keepdims=True))
        weights = (raised * (1.0 / jnp.sum(raised, axis=1, keepdims=True))).astype(BRAIN)
        weight_ref[pair] = weights.T
        context = dot(weights, values)
        context = jnp.where(low_lane, context[:ROWS], context[ROWS:])
        context_ref[:, at : at + LANES] = context.astype(BRAIN)
    attended = dot(context_ref[...], merge_ref[...]) + wide(adjust_ref)
    normal, inverse = normalized(x.astype(FLOAT_KIND) + attended)
    normal_ref[...] = normal
    inverse_ref[...] = inverse
    low_ref[...] = (normal * wide(gain_ref) + wide(shift_ref)).astype(BRAIN)


def attend(enc, x, project, offsets, segments, merge, adjust, gain, shift):
    count, width = x.shape
    blocks = count // ROWS
    heads = width // HEAD
    return pl.pallas_call(
        attend_kernel,
        grid_spec=pltpu.PrefetchScalarGridSpec(
            num_scalar_prefetch=1,
            grid=(blocks,),
            in_specs=[
                row_block(ROWS, width),
                whole(project.shape),
                whole(offsets.shape),
                pl.BlockSpec((1, ROWS), lambda i, *_: (0, i)),
                whole(merge.shape),
                whole(adjust.shape),
                whole(gain.shape),
                whole(shift.shape),
            ],
            out_specs=[
                row_block(ROWS, 3 * width),
                pl.BlockSpec((None, heads // 2, ROWS, 2 * ROWS), lambda i, *_: (i, 0, 0, 0)),
                row_block(ROWS, width),
                row_block(ROWS, width),
                row_block(ROWS, 1),
                row_block(ROWS, width),
            ],
        ),
        out_shape=[
            jax.ShapeDtypeStruct((count, 3 * width), BRAIN),
            jax.ShapeDtypeStruct((blocks, heads // 2, ROWS, 2 * ROWS), BRAIN),
            jax.ShapeDtypeStruct((count, width), BRAIN),
            jax.ShapeDtypeStruct((count, width), FLOAT_KIND),
            jax.ShapeDtypeStruct((count, 1), FLOAT_KIND),
            jax.ShapeDtypeStruct((count, width), BRAIN),
        ],
        cost_estimate=cost(1, 1),
        compiler_params=pltpu.CompilerParams(vmem_limit_bytes=17 * MEGA),
        name="attend",
    )(enc, x, project, offsets, segments, merge, adjust, gain, shift)


def summary_kernel(
    flag_ref,
    start_ref,
    target_ref,
    normal_ref,
    gain_one_ref,
    shift_one_ref,
    expand_ref,
    lift_ref,
    shrink_ref,
    settle_ref,
    gain_two_ref,
    shift_two_ref,
    out_ref,
    tile_ref,
    row_ref,
    low_ref,
    total_ref,
    copy_sem,
):
    slots, width = row_ref.shape
    step = pl.program_id(0)

    @pl.when(step == 0)
    def _():
        copies = [
            pltpu.make_async_copy(
                normal_ref.at[jnp.where(flag_ref[ENC] == 1, start_ref[slot], slot * QLEN) // TILE],
                tile_ref.at[slot],
                copy_sem.at[slot],
            )
            for slot in range(slots)
        ]
        for copy in copies:
            copy.start()
        for copy in copies:
            copy.wait()
        rows = tile_ref[:, 0, :] * wide(gain_one_ref) + wide(shift_one_ref)
        row_ref[...] = rows
        low_ref[...] = rows.astype(BRAIN)
        total_ref[...] = jnp.zeros_like(total_ref)

    activated, _ = gelu_and_slope(dot(low_ref[...], expand_ref[...]) + wide(lift_ref))
    total_ref[...] += dot(activated.astype(BRAIN), shrink_ref[...])

    @pl.when(step == pl.num_programs(0) - 1)
    def _():
        normal, _ = normalized(row_ref[...] + (total_ref[...] + wide(settle_ref)))
        out_ref[:, :width] = (normal * wide(gain_two_ref) + wide(shift_two_ref)).astype(BRAIN)
        lane = lax.broadcasted_iota(jnp.int32, (slots, LANES), 1)
        place = lax.broadcasted_iota(jnp.int32, (slots, LANES), 0)
        digits = jnp.zeros((slots, LANES), jnp.int32)
        for slot in range(slots):
            target = target_ref[slot]
            pair = jnp.where(lane == 0, target // LANES, jnp.where(lane == 1, target % LANES, 0))
            digits = jnp.where(place == slot, pair, digits)
        out_ref[:, width:] = digits.astype(FLOAT_KIND).astype(BRAIN)


def summarize(enc, starts, targets, normal, first, expand, lift, shrink, settle, second, tn=1024):
    count, width = normal.shape
    hidden = expand.shape[1]
    slots = starts.shape[0]
    row = whole((1, width))
    return pl.pallas_call(
        summary_kernel,
        grid_spec=pltpu.PrefetchScalarGridSpec(
            num_scalar_prefetch=3,
            grid=(hidden // tn,),
            in_specs=[
                pl.BlockSpec(memory_space=pl.ANY),
                row,
                row,
                pl.BlockSpec((width, tn), lambda i, *_: (0, i)),
                pl.BlockSpec((1, tn), lambda i, *_: (0, i)),
                pl.BlockSpec((tn, width), lambda i, *_: (i, 0)),
                row,
                row,
                row,
            ],
            out_specs=whole((slots, width + LANES)),
            scratch_shapes=[
                pltpu.VMEM((slots, TILE, width), FLOAT_KIND),
                pltpu.VMEM((slots, width), FLOAT_KIND),
                pltpu.VMEM((slots, width), BRAIN),
                pltpu.VMEM((slots, width), FLOAT_KIND),
                pltpu.SemaphoreType.DMA((slots,)),
            ],
        ),
        out_shape=jax.ShapeDtypeStruct((slots, width + LANES), BRAIN),
        cost_estimate=cost(1, 1),
        compiler_params=pltpu.CompilerParams(vmem_limit_bytes=10 * MEGA),
        name="summarize",
    )(
        enc,
        starts,
        targets,
        normal.reshape(count // TILE, TILE, width),
        *first,
        expand,
        lift,
        shrink,
        settle,
        *second,
    )


def widen_kernel(low_ref, expand_ref, lift_ref, *refs):
    active_ref, slope_ref = refs[-2:]

    @pl.loop(0, low_ref.shape[0] // ROWS)
    def _(block):
        rows = pl.ds(pl.multiple_of(block * ROWS, ROWS), ROWS)
        hidden = dot(low_ref[rows, :], expand_ref[...]) + wide(lift_ref)
        activated, slope = gelu_and_slope(hidden)
        active_ref[rows, :] = activated.astype(BRAIN)
        slope_ref[rows, :] = slope.astype(BRAIN)


def widen(part, parts, low, expand, lift, before, tn=768):
    count, width = low.shape
    hidden = expand.shape[1]
    steps = hidden // parts // tn
    column = lambda rows: pl.BlockSpec((rows, tn), lambda i: (0, part * steps + i))
    kept = [] if before is None else list(before)
    return pl.pallas_call(
        widen_kernel,
        grid=(steps,),
        in_specs=[whole(low.shape), column(width), column(1)]
        + [pl.BlockSpec(memory_space=pl.ANY)] * len(kept),
        out_specs=[column(count), column(count)],
        out_shape=[jax.ShapeDtypeStruct((count, hidden), BRAIN)] * 2,
        input_output_aliases={3 + k: k for k in range(len(kept))},
        cost_estimate=cost(1, 1),
        compiler_params=pltpu.CompilerParams(vmem_limit_bytes=10 * MEGA),
        name="widen",
    )(low, expand, lift, *kept)


def shrink_kernel(
    active_ref,
    shrink_ref,
    normal_ref,
    gain_one_ref,
    shift_one_ref,
    settle_ref,
    gain_two_ref,
    shift_two_ref,
    out_ref,
    inverse_ref,
    encoded_ref,
):
    normed = normal_ref[...] * wide(gain_one_ref) + wide(shift_one_ref)
    shrunk = dot(active_ref[...], shrink_ref[...]) + wide(settle_ref)
    normal, inverse = normalized(normed + shrunk)
    out_ref[...] = normal
    inverse_ref[...] = inverse
    encoded_ref[...] = (normal * wide(gain_two_ref) + wide(shift_two_ref)).astype(BRAIN)


def shrink_back_to_width(active, shrink, normal, first, settle, second, tm=256):
    count, hidden = active.shape
    width = shrink.shape[1]
    row = whole((1, width))
    return pl.pallas_call(
        shrink_kernel,
        grid=(count // tm,),
        in_specs=[row_block(tm, hidden), whole(shrink.shape), row_block(tm, width)] + [row] * 5,
        out_specs=[row_block(tm, width), row_block(tm, 1), row_block(tm, width)],
        out_shape=[
            jax.ShapeDtypeStruct((count, width), FLOAT_KIND),
            jax.ShapeDtypeStruct((count, 1), FLOAT_KIND),
            jax.ShapeDtypeStruct((count, width), BRAIN),
        ],
        cost_estimate=cost(1, 1),
        compiler_params=pltpu.CompilerParams(vmem_limit_bytes=14 * MEGA),
        name="shrink",
    )(active, shrink, normal, *first, settle, *second)


def contrast_kernel(
    flag_ref,
    start_ref,
    every_ref,
    column_ref,
    normal_ref,
    inverse_ref,
    cotangent_ref,
    gain_ref,
    two_ref,
    low_ref,
    sums_ref,
    summary_ref,
    rows_ref,
):
    width = normal_ref.shape[1]
    slots = start_ref.shape[0]
    devices = every_ref.shape[0]
    step = pl.program_id(0)
    sharpness = SHARPNESS_DIVISOR / math.sqrt(width)

    def flat(which, at, count):
        return every_ref[pl.ds(at, count), which].reshape(count * slots, width + LANES)

    def logits_of(questions, passages):
        return jnp.where(
            column_ref[...] >= 0, dot_rows(questions, passages) * sharpness, HIDDEN_SCORE
        )

    def targets_of(rows):
        digits = rows[:, width:].astype(FLOAT_KIND)
        return (digits[:, 0:1] * LANES + digits[:, 1:2]).astype(jnp.int32)

    @pl.when(step == 0)
    def _():
        sums_ref[...] = jnp.zeros_like(sums_ref)

        @pl.when(flag_ref[ENC] == 0)
        def _():
            own = every_ref[0, 0]
            passages = flat(1, 0, devices)[:, :width]
            logits = logits_of(own[:, :width], passages)
            top = jnp.max(logits, axis=1, keepdims=True)
            raised = jnp.exp(logits - top)
            probability = raised / jnp.sum(raised, axis=1, keepdims=True)
            hit = (column_ref[...] == targets_of(own)).astype(FLOAT_KIND)
            gradient = (LOSS_WEIGHT * (probability - hit)).astype(BRAIN)
            summary_ref[...] = dot(gradient, passages) * sharpness

        @pl.when(flag_ref[ENC] == 1)
        def _():
            passages = flat(0, 0, devices)[:, :width]
            block = 16

            def part(at):
                rows = flat(1, at, block)
                questions = rows[:, :width]
                logits = logits_of(questions, passages)
                top = jnp.max(logits, axis=1, keepdims=True)
                total = jnp.sum(jnp.exp(logits - top), axis=1, keepdims=True)
                probability = jnp.exp(logits[:, :LANES] - top) / total
                hit = (column_ref[:, :LANES] == targets_of(rows)).astype(FLOAT_KIND)
                gradient = (LOSS_WEIGHT * (probability - hit)).astype(BRAIN)
                return dot_columns(gradient, questions)[:slots] * sharpness

            if devices == block:
                summary_ref[...] = part(0)
            else:
                summary_ref[...] = jnp.zeros_like(summary_ref)

                @pl.loop(0, devices // block)
                def _(k):
                    summary_ref[...] += part(k * block)

    rows_ref[...] = wide(cotangent_ref)
    tiles = rows_ref.shape[0] // TILE
    first = lax.broadcasted_iota(jnp.int32, (TILE, 1), 0) == 0
    for slot in range(slots):
        start = jnp.where(flag_ref[ENC] == 1, start_ref[slot], slot * QLEN)
        local = start // TILE - step * tiles
        inside = (local >= 0) & (local < tiles)
        at = pl.multiple_of(jnp.clip(local, 0, tiles - 1) * TILE, TILE)
        rows_ref[pl.ds(at, TILE), :] += jnp.where(
            first & inside, summary_ref[slot : slot + 1, :], 0.0
        )
    gradient = rows_ref[...]
    normal = normal_ref[...]
    sums_ref[0:1] += row_sum(gradient * normal)
    sums_ref[1:2] += row_sum(gradient)
    two = norm_backward(gradient, normal, inverse_ref[...], wide(gain_ref))
    two_ref[...] = two
    low = two.astype(BRAIN)
    low_ref[...] = low
    sums_ref[2:3] += row_sum(low.astype(FLOAT_KIND))


def contrast(enc, starts, every, columns, normal, inverse, cotangent, gain, tm=256):
    count, width = normal.shape
    slots = starts.shape[0]
    return pl.pallas_call(
        contrast_kernel,
        grid_spec=pltpu.PrefetchScalarGridSpec(
            num_scalar_prefetch=2,
            grid=(count // tm,),
            in_specs=[
                whole(every.shape),
                whole(columns.shape),
                row_block(tm, width),
                row_block(tm, 1),
                row_block(tm, width),
                whole(gain.shape),
            ],
            out_specs=[row_block(tm, width), row_block(tm, width), whole((TILE, width))],
            scratch_shapes=[
                pltpu.VMEM((slots, width), FLOAT_KIND),
                pltpu.VMEM((tm, width), FLOAT_KIND),
            ],
        ),
        out_shape=[
            jax.ShapeDtypeStruct((count, width), FLOAT_KIND),
            jax.ShapeDtypeStruct((count, width), BRAIN),
            jax.ShapeDtypeStruct((TILE, width), FLOAT_KIND),
        ],
        cost_estimate=cost(1, 1),
        compiler_params=pltpu.CompilerParams(vmem_limit_bytes=8 * MEGA),
        name="contrast",
    )(enc, starts, every, columns, normal, inverse, cotangent, gain)


def contraction_kernel(flag_ref, low_ref, active_ref, *refs):
    turned_ref = refs[-1]
    step = pl.program_id(0)

    @pl.when(step == 0)
    def _():
        turned_ref[...] = low_ref[...].T

    value = dot(turned_ref[...], active_ref[...]).astype(BRAIN)
    for piece, out_ref in enumerate(refs[:-1]):

        @pl.when(step == piece)
        def _():
            out_ref[...] = value


def contraction_half(side, active, low, weight=1):
    count, hidden = active.shape
    width = low.shape[1]
    rows = width // 2
    tn = hidden // PIECES
    return pl.pallas_call(
        contraction_kernel,
        grid_spec=pltpu.PrefetchScalarGridSpec(
            num_scalar_prefetch=1,
            grid=(PIECES,),
            in_specs=[
                pl.BlockSpec((count, rows), lambda i, flag: (0, flag[0])),
                pl.BlockSpec((count, tn), lambda i, flag: (0, i)),
            ],
            out_specs=[whole((rows, tn))] * PIECES,
            scratch_shapes=[pltpu.VMEM((rows, count), BRAIN)],
        ),
        out_shape=[jax.ShapeDtypeStruct((rows, tn), BRAIN)] * PIECES,
        cost_estimate=cost(weight, 1),
        compiler_params=pltpu.CompilerParams(vmem_limit_bytes=8 * MEGA),
        name="contraction_half",
    )(side, low, active)


def feed_kernel(
    flag_ref,
    two_low_ref,
    shrink_ref,
    slope_ref,
    low_ref,
    expand_ref,
    two_ref,
    lift_ref,
    first_ref,
    *refs,
):
    pieces, turned_ref = refs[:-1], refs[-1]
    rows = turned_ref.shape[1]
    step = pl.program_id(0)

    @pl.when(step == 0)
    def _():
        first_ref[...] = two_ref[...]
        for side in range(2):

            @pl.when(flag_ref[SEND] == side)
            def _():
                turned_ref[0] = low_ref[:, side * rows : (side + 1) * rows].T
                turned_ref[1] = low_ref[:, (1 - side) * rows : (2 - side) * rows].T

    hidden = dot_rows(two_low_ref[...], shrink_ref[...]) * wide(slope_ref)
    low = hidden.astype(BRAIN)
    lift_ref[...] = row_sum(low.astype(FLOAT_KIND))
    first_ref[...] += dot_rows(low, expand_ref[...])
    for side in range(2):
        value = dot(turned_ref[side], low).astype(BRAIN)
        for piece in range(PIECES):

            @pl.when(step == piece)
            def _():
                pieces[side * PIECES + piece][...] = value


def feed_back(flags, two_low, shrink, slope, low, expand, two, weight=1):
    count, width = two.shape
    hidden = shrink.shape[0]
    rows = width // 2
    tn = hidden // PIECES
    column = lambda rows: pl.BlockSpec((rows, tn), lambda i, *_: (0, i))
    return pl.pallas_call(
        feed_kernel,
        grid_spec=pltpu.PrefetchScalarGridSpec(
            num_scalar_prefetch=1,
            grid=(PIECES,),
            in_specs=[
                whole((count, width)),
                row_block(tn, width),
                column(count),
                whole((count, width)),
                column(width),
                whole((count, width)),
            ],
            out_specs=[column(1), whole((count, width))] + [whole((rows, tn))] * 2 * PIECES,
            scratch_shapes=[pltpu.VMEM((2, rows, count), BRAIN)],
        ),
        out_shape=[
            jax.ShapeDtypeStruct((1, hidden), FLOAT_KIND),
            jax.ShapeDtypeStruct((count, width), FLOAT_KIND),
        ]
        + [jax.ShapeDtypeStruct((rows, tn), BRAIN)] * 2 * PIECES,
        cost_estimate=cost(weight, 1),
        compiler_params=pltpu.CompilerParams(vmem_limit_bytes=14 * MEGA),
        name="feed_back",
    )(flags, two_low, shrink, slope, low, expand, two)


def attend_back_kernel(
    first_ref,
    normal_ref,
    inverse_ref,
    gain_ref,
    merge_ref,
    packed_ref,
    weight_ref,
    one_ref,
    low_ref,
    packed_gradient_ref,
    sums_ref,
    packed_sums_ref,
    context_gradient_ref,
):
    width = normal_ref.shape[1]

    @pl.when(pl.program_id(0) == 0)
    def _():
        sums_ref[...] = jnp.zeros_like(sums_ref)
        packed_sums_ref[...] = jnp.zeros_like(packed_sums_ref)

    gradient = first_ref[...]
    normal = normal_ref[...]
    sums_ref[0:1] += row_sum(gradient * normal)
    sums_ref[1:2] += row_sum(gradient)
    one = norm_backward(gradient, normal, inverse_ref[...], wide(gain_ref))
    one_ref[...] = one
    low = one.astype(BRAIN)
    low_ref[...] = low
    sums_ref[2:3] += row_sum(low.astype(FLOAT_KIND))
    context_gradient_ref[...] = dot_rows(low, merge_ref[...]).astype(BRAIN)
    low_row = lax.broadcasted_iota(jnp.int32, (LANES, 1), 0) < HEAD
    scale = 1.0 / math.sqrt(HEAD)
    for pair in range(width // LANES):
        at = LANES * pair
        queries = both_heads(packed_ref[:, at : at + LANES] * scale)
        keys = packed_ref[:, width + at : width + at + LANES] * scale
        values = packed_ref[:, 2 * width + at : 2 * width + at + LANES]
        outer = both_heads(context_gradient_ref[:, at : at + LANES])
        weights = weight_ref[pair]
        probability = weights.astype(FLOAT_KIND)
        inner = dot_rows(values, outer)
        scores = (probability * (inner - row_sum(probability * inner))).astype(BRAIN)
        turned = dot(keys.T, scores)
        found = (
            jnp.where(low_row, turned[:, :ROWS], turned[:, ROWS:]).T,
            dot(scores, queries),
            dot(weights, outer),
        )
        for part in range(3):
            columns = slice(part * width + at, part * width + at + LANES)
            packed_gradient_ref[:, columns] = found[part].astype(BRAIN)
    packed_sums_ref[...] += row_sum(wide(packed_gradient_ref))


def attend_back(first, normal, inverse, gain, merge, packed, weights, weight=1):
    count, width = normal.shape
    heads = width // HEAD
    return pl.pallas_call(
        attend_back_kernel,
        grid=(count // ROWS,),
        in_specs=[
            row_block(ROWS, width),
            row_block(ROWS, width),
            row_block(ROWS, 1),
            whole(gain.shape),
            whole(merge.shape),
            row_block(ROWS, 3 * width),
            pl.BlockSpec((None, heads // 2, ROWS, 2 * ROWS), lambda i: (i, 0, 0, 0)),
        ],
        out_specs=[
            row_block(ROWS, width),
            row_block(ROWS, width),
            row_block(ROWS, 3 * width),
            whole((TILE, width)),
            whole((1, 3 * width)),
        ],
        out_shape=[
            jax.ShapeDtypeStruct((count, width), FLOAT_KIND),
            jax.ShapeDtypeStruct((count, width), BRAIN),
            jax.ShapeDtypeStruct((count, 3 * width), BRAIN),
            jax.ShapeDtypeStruct((TILE, width), FLOAT_KIND),
            jax.ShapeDtypeStruct((1, 3 * width), FLOAT_KIND),
        ],
        scratch_shapes=[pltpu.VMEM((ROWS, width), BRAIN)],
        cost_estimate=cost(weight, 1),
        compiler_params=pltpu.CompilerParams(vmem_limit_bytes=11 * MEGA),
        name="attend_back",
    )(first, normal, inverse, gain, merge, packed, weights)


def merge_project_kernel(flag_ref, context_ref, one_ref, x_ref, packed_ref, *refs):
    pieces, turned_ref = refs[:-1], refs[-1]
    step = pl.program_id(0)

    @pl.when(step == 0)
    def _():
        turned_ref[...] = context_ref[...].T
        pieces[0][...] = dot(turned_ref[...], one_ref[...]).astype(BRAIN)
        turned_ref[...] = x_ref[...].T

    @pl.when(step > 0)
    def _():
        value = dot(turned_ref[...], packed_ref[...]).astype(BRAIN)
        for piece in range(1, PIECES):

            @pl.when(step == piece)
            def _():
                pieces[piece][...] = value


def merge_project_half(side, context, one, x, packed, weight=1):
    count, width = x.shape
    rows = width // 2
    return pl.pallas_call(
        merge_project_kernel,
        grid_spec=pltpu.PrefetchScalarGridSpec(
            num_scalar_prefetch=1,
            grid=(PIECES,),
            in_specs=[
                pl.BlockSpec((count, rows), lambda i, flag: (0, flag[0])),
                whole((count, width)),
                pl.BlockSpec((count, rows), lambda i, flag: (0, flag[0])),
                pl.BlockSpec((count, width), lambda i, flag: (0, jnp.maximum(i - 1, 0))),
            ],
            out_specs=[whole((rows, width))] * PIECES,
            scratch_shapes=[pltpu.VMEM((rows, count), BRAIN)],
        ),
        out_shape=[jax.ShapeDtypeStruct((rows, width), BRAIN)] * PIECES,
        cost_estimate=cost(weight, 1),
        compiler_params=pltpu.CompilerParams(vmem_limit_bytes=10 * MEGA),
        name="merge_project_half",
    )(side, context, one, x, packed)


def fold_kernel(flag_ref, *refs, count, side):
    keep, other, outs = refs[:count], refs[count : 2 * count], refs[2 * count :]
    rows = outs[0].shape[0]
    columns = outs[0].shape[1] // count
    for out_ref, half in zip(outs, (1 - flag_ref[side], flag_ref[side])):

        @pl.loop(0, rows // PACKED)
        def _(block):
            to = pl.ds(pl.multiple_of(block * PACKED, PACKED), PACKED)
            at = pl.ds(pl.multiple_of(half * rows + block * PACKED, PACKED), PACKED)
            for piece in range(count):
                total = wide(keep[piece].at[at]) + wide(other[piece].at[at])
                out_ref[to, piece * columns : (piece + 1) * columns] = total.astype(BRAIN)


def folded(flags, place, keep, other, weight):
    rows, columns = keep[0].shape
    count = len(keep)
    if rows % (2 * PACKED):
        (mine,), (theirs,) = keep, other
        bit = flags[place]
        return part_sum(mine, theirs, 1 - bit), part_sum(mine, theirs, bit)
    shape = jax.ShapeDtypeStruct((rows // 2, count * columns), BRAIN)
    return pl.pallas_call(
        functools.partial(fold_kernel, count=count, side=place),
        grid_spec=pltpu.PrefetchScalarGridSpec(
            num_scalar_prefetch=1,
            grid=(1,),
            in_specs=[whole((rows, columns))] * 2 * count,
            out_specs=[whole(shape.shape)] * 2,
        ),
        out_shape=[shape, shape],
        cost_estimate=cost(weight, 1),
        compiler_params=pltpu.CompilerParams(vmem_limit_bytes=5 * MEGA),
        name="fold",
    )(flags, *keep, *other)


def add_kernel(mine_ref, other_ref, out_ref):
    out_ref[...] = (wide(mine_ref) + wide(other_ref)).astype(out_ref.dtype)


def added(mine, other, weight=1):
    return pl.pallas_call(
        add_kernel,
        out_shape=jax.ShapeDtypeStruct(mine.shape, mine.dtype),
        cost_estimate=cost(weight, 1),
        compiler_params=pltpu.CompilerParams(vmem_limit_bytes=2 * MEGA),
        name="add",
    )(mine, other)


def join_kernel(flag_ref, mine_ref, other_ref, out_ref, *, side):
    rows = mine_ref.shape[0]
    out_ref[pl.ds(pl.multiple_of(flag_ref[side] * rows, rows), rows), :] = mine_ref[...]
    out_ref[pl.ds(pl.multiple_of((1 - flag_ref[side]) * rows, rows), rows), :] = other_ref[...]


def joined(flags, place, mine, other, weight):
    rows, columns = mine.shape
    if rows % PACKED:
        return joined_by_bit(mine, other, flags[place])
    return pl.pallas_call(
        functools.partial(join_kernel, side=place),
        grid_spec=pltpu.PrefetchScalarGridSpec(
            num_scalar_prefetch=1,
            grid=(1,),
            in_specs=[whole(mine.shape)] * 2,
            out_specs=whole((2 * rows, columns)),
        ),
        out_shape=jax.ShapeDtypeStruct((2 * rows, columns), BRAIN),
        cost_estimate=cost(weight, 1),
        compiler_params=pltpu.CompilerParams(vmem_limit_bytes=4 * MEGA),
        name="join",
    )(flags, mine, other)


def tokens_kernel(one_ref, packed_ref, project_ref, out_ref):
    out_ref[...] = one_ref[...] + dot_rows(packed_ref[...], project_ref[...])


def tokens_back(one, packed, project, tm=256, weight=1):
    count, width = one.shape
    return pl.pallas_call(
        tokens_kernel,
        grid=(count // tm,),
        in_specs=[row_block(tm, width), row_block(tm, 3 * width), whole(project.shape)],
        out_specs=row_block(tm, width),
        out_shape=jax.ShapeDtypeStruct((count, width), FLOAT_KIND),
        cost_estimate=cost(weight, 1),
        compiler_params=pltpu.CompilerParams(vmem_limit_bytes=13 * MEGA),
        name="tokens_back",
    )(one, packed, project)


def pack_kernel(packed_ref, attend_ref, lift_ref, output_ref, out_ref):
    width = attend_ref.shape[1]
    out_ref[...] = jnp.zeros_like(out_ref)
    out_ref[0:1] = packed_ref[:, :width]
    out_ref[1:2] = packed_ref[:, 2 * width :]
    out_ref[2:5] = attend_ref[0:3]
    for part in range(4):
        out_ref[5 + part : 6 + part] = lift_ref[:, part * width : (part + 1) * width]
    out_ref[9:12] = output_ref[0:3]


def pack_vectors(packed_sums, attend_sums, lift_sums, output_sums):
    width = attend_sums.shape[1]
    return pl.pallas_call(
        pack_kernel,
        out_shape=jax.ShapeDtypeStruct((16, width), FLOAT_KIND),
        cost_estimate=cost(1, 1),
        compiler_params=pltpu.CompilerParams(vmem_limit_bytes=2 * MEGA),
        name="pack_vectors",
    )(packed_sums, attend_sums, lift_sums, output_sums)


def unpack_kernel(mine_ref, other_ref, offset_ref, adjust_ref, scale_ref, center_ref, lift_ref, settle_ref, rescale_ref, recenter_ref):
    width = mine_ref.shape[1]
    total = mine_ref[...] + other_ref[...]
    offset_ref[:, :width] = total[0:1]
    offset_ref[:, width:] = total[1:2]
    scale_ref[...] = total[2:3]
    center_ref[...] = total[3:4]
    adjust_ref[...] = total[4:5]
    for part in range(4):
        lift_ref[:, part * width : (part + 1) * width] = total[5 + part : 6 + part]
    rescale_ref[...] = total[9:10]
    recenter_ref[...] = total[10:11]
    settle_ref[...] = total[11:12]


def unpack_vectors(mine, other):
    width = mine.shape[1]
    shapes = [2, 1, 1, 1, 4, 1, 1, 1]
    return pl.pallas_call(
        unpack_kernel,
        out_shape=[jax.ShapeDtypeStruct((1, k * width), FLOAT_KIND) for k in shapes],
        cost_estimate=cost(1, 1),
        compiler_params=pltpu.CompilerParams(vmem_limit_bytes=2 * MEGA),
        name="unpack_vectors",
    )(mine, other)


def place_kernel(flag_ref, value_ref, *refs, kept):
    at = 0
    for out_ref in refs[kept:]:
        columns = out_ref.shape[1]
        out_ref[...] = value_ref[:, at : at + columns].astype(FLOAT_KIND)
        at += columns


def place_half(flags, side, value, columns, before, tm=192):
    rows = value.shape[0]
    steps = rows // tm
    kept = [] if before is None else list(before)
    return pl.pallas_call(
        functools.partial(place_kernel, kept=len(kept)),
        grid_spec=pltpu.PrefetchScalarGridSpec(
            num_scalar_prefetch=1,
            grid=(steps,),
            in_specs=[row_block(tm, value.shape[1])]
            + [pl.BlockSpec(memory_space=pl.ANY)] * len(kept),
            out_specs=[
                pl.BlockSpec((tm, size), lambda i, flag: (flag[side] * steps + i, 0))
                for size in columns
            ],
        ),
        out_shape=[jax.ShapeDtypeStruct((2 * rows, size), FLOAT_KIND) for size in columns],
        input_output_aliases={2 + k: k for k in range(len(kept))},
        cost_estimate=cost(1, 1),
        compiler_params=pltpu.CompilerParams(vmem_limit_bytes=10 * MEGA),
        name="place_half",
    )(flags, value, *kept)


def place_turned_kernel(flag_ref, value_ref, *refs):
    refs[-1][...] = value_ref[...].astype(FLOAT_KIND).T


def place_turned_half(flags, side, value, before, tm=1536):
    rows, columns = value.shape
    kept = [] if before is None else list(before)
    return pl.pallas_call(
        place_turned_kernel,
        grid_spec=pltpu.PrefetchScalarGridSpec(
            num_scalar_prefetch=1,
            grid=(columns // tm,),
            in_specs=[pl.BlockSpec((rows, tm), lambda i, flag: (0, i))]
            + [pl.BlockSpec(memory_space=pl.ANY)] * len(kept),
            out_specs=[pl.BlockSpec((tm, rows), lambda i, flag: (i, flag[side]))],
        ),
        out_shape=[jax.ShapeDtypeStruct((columns, 2 * rows), FLOAT_KIND)],
        input_output_aliases={2 + k: k for k in range(len(kept))},
        cost_estimate=cost(1, 1),
        compiler_params=pltpu.CompilerParams(vmem_limit_bytes=14 * MEGA),
        name="place_turned_half",
    )(flags, value, *kept)


def swapped(value, axis, apart):
    mask = 2**apart
    pairs = [(source, source ^ mask) for source in range(lax.axis_size(axis))]
    return lax.ppermute(value, axis, pairs)


def swapped_by_core(value, stage):
    count = lax.axis_size("batch")
    pairs = [(source, source ^ (1 << stage[source & 1])) for source in range(count)]
    return lax.ppermute(value, "batch", pairs)


def bit_count(axis):
    return lax.axis_size(axis).bit_length() - 1


def to_low(values):
    return values.astype(BRAIN)


def part_sum(mine, other, bit):
    half = mine.shape[0] // 2
    left = lax.dynamic_slice_in_dim(mine, bit * half, half, 0).astype(FLOAT_KIND)
    right = lax.dynamic_slice_in_dim(other, bit * half, half, 0).astype(FLOAT_KIND)
    return to_low(left + right)


def joined_by_bit(mine, other, bit):
    low_part = jnp.where(bit == 0, mine, other)
    high_part = jnp.where(bit == 0, other, mine)
    return jnp.concatenate([low_part, high_part], axis=0)


class Sequence:
    def __init__(self):
        self.last = None

    def run(self, step, *inputs):
        if self.last is not None:
            *inputs, _ = lax.optimization_barrier((*inputs, self.last))
        result = step(*inputs)
        self.last = jax.tree.leaves(result)[0]
        return result


class Reduction:
    def __init__(self, sequence, flags, stages, at, put):
        self.run = sequence.run
        self.flags = flags
        self.stages = stages
        self.at = at
        self.put = put
        count = len(stages)
        self.steps = [functools.partial(self.scatter, k) for k in range(count)]
        self.steps.append(self.finish)
        self.steps += [functools.partial(self.gather, k) for k in reversed(range(count))]
        self.steps.append(self.place)

    def advance(self, weight=1):
        self.steps.pop(0)(weight)

    def begin(self, send, keep):
        self.keep = list(keep)
        self.other = [swapped(piece, "batch", 0) for piece in send]

    def scatter(self, stage, weight):
        count = len(self.keep)
        send, keep = self.run(
            lambda *v: folded(self.flags, self.at + stage, v[:count], v[count:], weight),
            *self.keep,
            *self.other,
        )
        self.keep = [keep]
        self.other = [swapped_by_core(send, self.stages[stage])]

    def finish(self, weight):
        self.value = self.run(lambda a, b: added(a, b, weight), *self.keep, *self.other)
        self.other = swapped_by_core(self.value, self.stages[-1])

    def gather(self, stage, weight):
        self.value = self.run(
            lambda v, o: joined(self.flags, self.at + stage, v, o, weight), self.value, self.other
        )
        if stage > 0:
            self.other = swapped_by_core(self.value, self.stages[stage - 1])
            return
        self.other = swapped(self.value, "batch", 0)
        self.placed = self.run(lambda v: self.put(self.flags, KEEP, v, None), self.value)

    def place(self, weight):
        self.total = self.run(
            lambda o, *p: self.put(self.flags, SEND, o, p), self.other, *self.placed
        )


def shards(
    tokens,
    cotangent,
    projection,
    offsets,
    merger,
    adjust,
    scaling,
    centering,
    expansion,
    lifting,
    contraction,
    settling,
    rescale,
    recenter,
    segments,
    passage_starts,
    passage_counts,
    positives,
):
    index = lax.axis_index("batch").astype(jnp.int32)
    slots = passage_starts.shape[0]
    bits = bit_count("batch")
    plain = [(apart, apart) for apart in range(1, bits)]
    mixed = [(apart, other) for (apart, _), (other, _) in zip(plain, plain[1:] + plain[:1])]
    kinds = (plain, mixed, [(odd, even) for even, odd in mixed])
    flags = jnp.stack(
        [lax.axis_index("enc").astype(jnp.int32), index & 1, 1 - (index & 1)]
        + [
            (index >> jnp.where(index & 1 == 0, even, odd)) & 1
            for stages in kinds
            for even, odd in stages
        ]
    )
    order = list(reversed(range(bits)))
    place = jnp.arange(lax.axis_size("batch"), dtype=jnp.int32)
    away = sum(((place >> k) & 1) << apart for k, apart in enumerate(order))
    device = (index ^ away)[:, None]
    slot = jnp.arange(slots, dtype=jnp.int32)[None, :]
    held = jnp.sum(jnp.where(device == place[None, :], passage_counts[None, :], 0), axis=1)
    columns = jnp.where(slot < held[:, None], device * slots + slot, -1).reshape(1, -1)
    keep_side = (index & 1)[None]
    flags, keep_side, send_side, columns, tokens = lax.optimization_barrier(
        (flags, keep_side, 1 - keep_side, columns, tokens)
    )
    width = tokens.shape[2]
    x, project, merge, expand, shrink, outer = (
        in_hbm(tokens[0]),
        in_hbm(projection[0]),
        in_hbm(merger[0]),
        expansion[0],
        in_hbm(contraction[0]),
        in_hbm(cotangent[0]),
    )
    first = (in_hbm(scaling), in_hbm(centering))
    second = (in_hbm(rescale), in_hbm(recenter))
    adjust, lifting, settling, offsets = (
        in_hbm(v) for v in (adjust, lifting, settling, offsets)
    )

    sequence = Sequence()
    run = sequence.run
    packed, weights, context, normal_one, inverse_one, low = attend(
        flags, x, project, offsets, in_hbm(segments[None]), merge, adjust, *first
    )
    parcel = summarize(
        flags,
        passage_starts,
        positives,
        normal_one,
        first,
        expand,
        lifting,
        shrink,
        settling,
        second,
    )
    sequence.last = parcel
    parts = 4
    every = parcel[None]
    other = swapped(parcel, "enc", 0)[None]
    wide_pair = run(lambda v: widen(0, parts, v, expand, lifting, None), low)
    every = run(lambda a, b: jnp.stack([a, b], axis=1), every, other)
    for part, apart in enumerate(order, 1):
        other = swapped(every, "batch", apart)
        if part < parts:
            wide_pair = run(
                lambda v, *p: widen(part, parts, v, expand, lifting, p), low, *wide_pair
            )
        elif part == parts:
            active, slope = wide_pair
            normal_two, inverse_two, encoded = run(
                lambda a, n: shrink_back_to_width(a, shrink, n, first, settling, second),
                active,
                normal_one,
            )
        every = run(lambda a, b: jnp.concatenate([a, b], axis=0), every, other)
    two, two_low, output_sums = run(
        lambda *v: contrast(flags, passage_starts, *v, outer, second[0]),
        every,
        columns,
        normal_two,
        inverse_two,
    )

    puts = (
        place_turned_half,
        lambda f, s, v, p: place_half(f, s, v, (expansion.shape[2],), p),
        lambda f, s, v, p: place_half(f, s, v, (width, projection.shape[2]), p),
    )
    shrink_sum, expand_sum, project_sum = (
        Reduction(sequence, flags, kinds[kind], STAGES + kind * len(plain), put)
        for kind, put in zip(LINKS, puts)
    )
    product = lambda side: run(
        lambda c, o, p: merge_project_half(side, c, o, x, p, weight),
        context,
        one_low,
        packed_gradient,
    )
    vectors = []
    apart = 0
    for step in PLAN:
        weight = LEVELS[int(step[1:] or 0)]
        kind = step[0]
        if kind == "C":
            send = run(lambda a, t: contraction_half(send_side, a, t, weight), active, two_low)
            keep = run(lambda a, t: contraction_half(keep_side, a, t, weight), active, two_low)
            shrink_sum.begin(send, keep)
        elif kind == "F":
            lift_sums, gradient_first, *both = run(
                lambda t, s, g: feed_back(flags, t, shrink, s, low, expand, g, weight),
                two_low,
                slope,
                two,
            )
            expand_sum.begin(both[:PIECES], both[PIECES:])
        elif kind == "A":
            one, one_low, packed_gradient, attend_sums, packed_sums = run(
                lambda g, n, i, p, w: attend_back(g, n, i, first[0], merge, p, w, weight),
                gradient_first,
                normal_one,
                inverse_one,
                packed,
                weights,
            )
        elif kind == "S":
            send = product(send_side)
        elif kind == "K":
            keep = product(keep_side)
            project_sum.begin(send, keep)
        elif kind == "T":
            tokens_gradient = run(lambda o, p: tokens_back(o, p, project, weight=weight), one, packed_gradient)
        elif kind == "P":
            vectors = [run(pack_vectors, packed_sums, attend_sums, lift_sums, output_sums)]
            vectors.append(swapped(vectors[0], "batch", apart))
        elif kind == "v":
            apart += 1
            vectors = [run(lambda a, b, w=weight: added(a, b, w), *vectors)]
            vectors.append(swapped(vectors[0], "batch", apart))
        else:
            {"c": shrink_sum, "e": expand_sum, "m": project_sum}[kind].advance(weight)
    while apart < bits - 1:
        apart += 1
        vectors = [run(added, *vectors)]
        vectors.append(swapped(vectors[0], "batch", apart))
    vector_totals = run(unpack_vectors, *vectors)
    for reduction in (shrink_sum, expand_sum, project_sum):
        while reduction.steps:
            reduction.advance()
    (total_contraction,) = shrink_sum.total
    (total_expansion,) = expand_sum.total
    total_merger, total_projection = project_sum.total
    (
        total_offsets,
        total_adjust,
        total_scaling,
        total_centering,
        total_lifting,
        total_settling,
        total_rescale,
        total_recenter,
    ) = vector_totals
    return (
        encoded[None],
        tokens_gradient[None],
        total_projection[None],
        total_offsets,
        total_merger[None],
        total_adjust,
        total_scaling,
        total_centering,
        total_expansion[None],
        total_lifting,
        total_contraction[None],
        total_settling,
        total_rescale,
        total_recenter,
    )


def solution(mesh):
    matrix = P("enc", None, None)
    vector = P("enc", None)
    rows = P("enc", "batch", None)
    return jax.shard_map(
        shards,
        mesh=mesh,
        in_specs=(
            rows,
            rows,
            matrix,
            vector,
            matrix,
            vector,
            vector,
            vector,
            matrix,
            vector,
            matrix,
            vector,
            vector,
            vector,
            P("batch"),
            P("batch"),
            P(),
            P("batch"),
        ),
        out_specs=(
            rows,
            rows,
            matrix,
            vector,
            matrix,
            vector,
            vector,
            vector,
            matrix,
            vector,
            matrix,
            vector,
            vector,
            vector,
        ),
        check_vma=False,
    )
```

profile of v0, /device:TPU:0, one launch (start us, length us, event | category | flops | bytes accessed | tf_op | source)
XLA Modules:
  0.0 303.6 jit_solution(1019585087553820095)
XLA Ops:
  1.9 17.6 %attend.1 = (bf16[1024,2304]{1,0:T(8,128)(2,1)S(1)}, bf16[4,6,256,512]{3,2,1,0:T(8,128)(2,1)S(1)}, bf16[1024,768]{1,0:T(8,128)(2,1)S(1)}, f32[1024,768]{1,0:T(8,...) custom-call(s32[12]{0:T(128)S(1)} %stack.60.flag_ref, bf16[1024,768]{1,0:T(8,128)(2,1)} %bitcast.49, ...), custom_call_target="tpu_custom_call" | custom-call | flops 1 | bytes 1 | tf_op jit(solution)/shard_map/attend/pallas_call | solution.py:173
  19.5 5.9 %summarize.1 = bf16[16,896]{1,0:T(8,128)(2,1)S(1)} custom-call(s32[12]{0:T(128)S(1)} %stack.60.flag_ref, s32[16]{0:T(128)S(1)} %copy-done.4, s32[16]{0:T(128)S(1)} %copy-done.5, f32[128,8,768]{2,1,0:T(8,128)S(1)} %bitcast.36, bf16[1,768]{1,0:T(2,128)(2,1)} %gain_ref.5, bf16[1,768]{1,0:T(2,128)(2,1)} %shift_one_ref.3, bf16[768,3072]{1,0:T(8,128)(2,1)S(1)} %bitcast.30, ...), custom_call_target="tpu_custom_call" | custom-call | flops 1 | bytes 1 | tf_op jit(solution)/shard_map/summarize/pallas_call | solution.py:275
  25.4 3.0 collective-permute-start
  28.4 4.9 %widen.4 = (bf16[1024,3072]{1,0:T(8,128)(2,1)S(1)}, bf16[1024,3072]{1,0:T(8,128)(2,1)S(1)}) custom-call(bf16[1024,768]{1,0:T(8,128)(2,1)S(1)} %get-tuple-element.251.low_ref, bf16[768,3072]{1,0:T(8,128)(2,1)S(1)} %bitcast.31, bf16[1,3072]{1,0:T(2,128)(2,1)} %lift_ref.9), custom_call_target="tpu_custom_call" | custom-call | flops 1 | bytes 1 | tf_op jit(solution)/shard_map/widen/pallas_call | solution.py:336
  36.0 4.9 %widen.5 = (bf16[1024,3072]{1,0:T(8,128)(2,1)S(1)}, bf16[1024,3072]{1,0:T(8,128)(2,1)S(1)}) custom-call(bf16[1024,768]{1,0:T(8,128)(2,1)S(1)} %get-tuple-element.251.low_ref, bf16[768,3072]{1,0:T(8,128)(2,1)S(1)} %bitcast.32, bf16[1,3072]{1,0:T(2,128)(2,1)} %lift_ref.9, ...), custom_call_target="tpu_custom_call", output_to_operand_aliasing={{0}: (3, {}), {1}: (4, {})} | custom-call | flops 1 | bytes 1 | tf_op jit(solution)/shard_map/widen/pallas_call | solution.py:336
  42.6 4.9 %widen.6 = (bf16[1024,3072]{1,0:T(8,128)(2,1)S(1)}, bf16[1024,3072]{1,0:T(8,128)(2,1)S(1)}) custom-call(bf16[1024,768]{1,0:T(8,128)(2,1)S(1)} %get-tuple-element.251.low_ref, bf16[768,3072]{1,0:T(8,128)(2,1)S(1)} %bitcast.33, bf16[1,3072]{1,0:T(2,128)(2,1)} %lift_ref.9, ...), custom_call_target="tpu_custom_call", output_to_operand_aliasing={{0}: (3, {}), {1}: (4, {})} | custom-call | flops 1 | bytes 1 | tf_op jit(solution)/shard_map/widen/pallas_call | solution.py:336
  49.1 4.9 %widen.7 = (bf16[1024,3072]{1,0:T(8,128)(2,1)S(1)}, bf16[1024,3072]{1,0:T(8,128)(2,1)S(1)}) custom-call(bf16[1024,768]{1,0:T(8,128)(2,1)S(1)} %get-tuple-element.251.low_ref, bf16[768,3072]{1,0:T(8,128)(2,1)S(1)} %bitcast.34, bf16[1,3072]{1,0:T(2,128)(2,1)} %lift_ref.9, ...), custom_call_target="tpu_custom_call", output_to_operand_aliasing={{0}: (3, {}), {1}: (4, {})} | custom-call | flops 1 | bytes 1 | tf_op jit(solution)/shard_map/widen/pallas_call | solution.py:336
  56.8 9.8 %shrink.1 = (f32[1024,768]{1,0:T(8,128)S(1)}, f32[1024,1]{1,0:T(8,128)S(1)}, bf16[1024,768]{1,0:T(8,128)(2,1)}) custom-call(bf16[1024,3072]{1,0:T(8,128)(2,1)S(1)} %get-tuple-element.278.active_ref, bf16[3072,768]{1,0:T(8,128)(2,1)} %bitcast.41, f32[1024,768]{1,0:T(8,128)S(1)} %get-tuple-element.325.normal_ref, bf16[1,768]{1,0:T(2,128)(2,1)} %gain_ref.5, ...), custom_call_target="tpu_custom_call" | custom-call | flops 1 | bytes 1 | tf_op jit(solution)/shard_map/shrink/pallas_call | solution.py:375
  66.7 5.5 %contrast.1 = (f32[1024,768]{1,0:T(8,128)S(1)}, bf16[1024,768]{1,0:T(8,128)(2,1)S(1)}, f32[8,768]{1,0:T(8,128)S(1)}) custom-call(s32[12]{0:T(128)S(1)} %stack.60.flag_ref, s32[16]{0:T(128)S(1)} %copy-done.4, bf16[16,2,16,896]{3,2,1,0:T(8,128)(2,1)S(1)} %pad_maximum_fusion.every_ref, s32[1,256]{1,0:T(1,128)S(1)} %select_n.48.column_ref, ...), custom_call_target="tpu_custom_call" | custom-call | flops 1 | bytes 1 | tf_op jit(solution)/shard_map/contrast/pallas_call | solution.py:490
  72.2 4.2 %contraction_half.2 = (bf16[384,768]{1,0:T(8,128)(2,1)S(1)}, bf16[384,768]{1,0:T(8,128)(2,1)S(1)}, bf16[384,768]{1,0:T(8,128)(2,1)S(1)}, bf16[384,768]{1,0:T(8,128)(2,1)S(1)}) custom-call(s32[1]{0:T(128)S(6)} %sub.7.flag_ref, bf16[1024,768]{1,0:T(8,128)(2,1)S(1)} %get-tuple-element.295.low_ref.two_low_ref, bf16[1024,3072]{1,0:T(8,128)(2,1)S(1)} %get-tuple-element.278.active_ref), custom_call_target="tpu_custom_call" | custom-call | flops 99999997952 | bytes 1 | tf_op jit(solution)/shard_map/contraction_half/pallas_call | solution.py:541
  77.6 4.2 %contraction_half.3 = (bf16[384,768]{1,0:T(8,128)(2,1)S(1)}, bf16[384,768]{1,0:T(8,128)(2,1)S(1)}, bf16[384,768]{1,0:T(8,128)(2,1)S(1)}, bf16[384,768]{1,0:T(8,128)(2,1)S(1)}) custom-call(s32[1]{0:T(128)} %bitcast.1.flag_ref, bf16[1024,768]{1,0:T(8,128)(2,1)S(1)} %get-tuple-element.295.low_ref.two_low_ref, bf16[1024,3072]{1,0:T(8,128)(2,1)S(1)} %get-tuple-element.278.active_ref), custom_call_target="tpu_custom_call" | custom-call | flops 99999997952 | bytes 1 | tf_op jit(solution)/shard_map/contraction_half/pallas_call | solution.py:541
  84.2 21.4 %feed_back.1 = (f32[1,3072]{1,0:T(1,128)S(1)}, f32[1024,768]{1,0:T(8,128)S(1)}, bf16[384,768]{1,0:T(8,128)(2,1)S(1)}, bf16[384,768]{1,0:T(8,128)(2,1)S(1)}, bf16...) custom-call(s32[12]{0:T(128)S(1)} %stack.60.flag_ref, ...), custom_call_target="tpu_custom_call" | custom-call | flops 6000000000 | bytes 1 | tf_op jit(solution)/shard_map/feed_back/pallas_call | solution.py:605
  112.5 16.2 %attend_back.1 = (f32[1024,768]{1,0:T(8,128)S(1)}, bf16[1024,768]{1,0:T(8,128)(2,1)S(1)}, bf16[1024,2304]{1,0:T(8,128)(2,1)S(1)}, f32[8,768]{1,0:T(8,128)S(1)}, f32[1,2304]{1,0:T(1,128)S(1)}) custom-call(f32[1024,768]{1,0:T(8,128)S(1)} %get-tuple-element.324.first_ref, f32[1024,768]{1,0:T(8,128)S(1)} %get-tuple-element.325.normal_ref, ...), custom_call_target="tpu_custom_call" | custom-call | flops 6000000000 | bytes 1 | tf_op jit(solution)/shard_map/attend_back/pallas_call | solution.py:691
  130.0 5.0 %merge_project_half.2 = (bf16[384,768]{1,0:T(8,128)(2,1)S(1)}, bf16[384,768]{1,0:T(8,128)(2,1)S(1)}, bf16[384,768]{1,0:T(8,128)(2,1)S(1)}, bf16[384,768]{1,0:T(8,128)(2,1)S(1)}) custom-call(s32[1]{0:T(128)S(6)} %sub.7.flag_ref, bf16[1024,768]{1,0:T(8,128)(2,1)S(1)} %get-tuple-element.356.context_ref, bf16[1024,768]{1,0:T(8,128)(2,1)S(1)} %get-tuple-element.357.one_ref, ...), custom_call_target="tpu_custom_call" | custom-call | flops 20000000000 | bytes 1 | tf_op jit(solution)/shard_map/merge_project_half/pallas_call | solution.py:747
  135.7 3.3 %collective-permute-done.14.refs_1_ = bf16[192,3072]{1,0:T(8,128)(2,1)S(1)} collective-permute-done((bf16[192,3072]{1,0:T(8,128)(2,1)S(1)}, bf16[192,3072]{1,0:T(8,128)(2,1)S(1)}, u32[]{:S(2)}, u32[]{:S(2)}) %collective-permute-start.14) | collective-permute-done | bytes 1179680 | tf_op jit(solution)/shard_map/ppermute | solution.py:977
  140.9 5.0 %merge_project_half.3 = (bf16[384,768]{1,0:T(8,128)(2,1)S(1)}, bf16[384,768]{1,0:T(8,128)(2,1)S(1)}, bf16[384,768]{1,0:T(8,128)(2,1)S(1)}, bf16[384,768]{1,0:T(8,128)(2,1)S(1)}) custom-call(s32[1]{0:T(128)} %bitcast.1.flag_ref, bf16[1024,768]{1,0:T(8,128)(2,1)S(1)} %get-tuple-element.356.context_ref, bf16[1024,768]{1,0:T(8,128)(2,1)S(1)} %get-tuple-element.357.one_ref, ...), custom_call_target="tpu_custom_call" | custom-call | flops 20000000000 | bytes 1 | tf_op jit(solution)/shard_map/merge_project_half/pallas_call | solution.py:747
  149.3 17.3 %collective-permute-done.16.refs_1_ = bf16[96,3072]{1,0:T(8,128)(2,1)S(1)} collective-permute-done((bf16[96,3072]{1,0:T(8,128)(2,1)S(1)}, bf16[96,3072]{1,0:T(8,128)(2,1)S(1)}, u32[]{:S(2)}, u32[]{:S(2)}) %collective-permute-start.16) | collective-permute-done | bytes 589856 | tf_op jit(solution)/shard_map/ppermute | solution.py:977
  168.0 7.4 %tokens_back.1 = f32[1024,768]{1,0:T(8,128)} custom-call(f32[1024,768]{1,0:T(8,128)S(1)} %get-tuple-element.378.one_ref, bf16[1024,2304]{1,0:T(8,128)(2,1)S(1)} %get-tuple-element.379.packed_ref, bf16[768,2304]{1,0:T(8,128)(2,1)} %bitcast.44), custom_call_target="tpu_custom_call" | custom-call | flops 1 | bytes 1 | tf_op jit(solution)/shard_map/tokens_back/pallas_call | solution.py:851
  176.2 3.3 %collective-permute-done.22.refs_1_ = bf16[192,3072]{1,0:T(8,128)(2,1)S(1)} collective-permute-done((bf16[192,3072]{1,0:T(8,128)(2,1)S(1)}, bf16[192,3072]{1,0:T(8,128)(2,1)S(1)}, u32[]{:S(2)}, u32[]{:S(2)}) %collective-permute-start.22) | collective-permute-done | bytes 1179680 | tf_op jit(solution)/shard_map/ppermute | solution.py:977
  180.4 5.6 %collective-permute-start.26 = (bf16[96,3072]{1,0:T(8,128)(2,1)S(1)}, bf16[96,3072]{1,0:T(8,128)(2,1)S(1)}, u32[]{:S(2)}, u32[]{:S(2)}) collective-permute-start(bf16[96,3072]{1,0:T(8,128)(2,1)S(1)} %get-tuple-element.391), channel_id=1, source_target_pairs={{0,8},{1,5},{2,10},{3,7},{4,12},{5,1},{6,14},{7,3},{8,0},{9,13},{1... | collective-permute-start | bytes 1769480 | tf_op jit(solution)/shard_map/ppermute | solution.py:977
  186.0 22.1 %collective-permute-done.27.other_ref = bf16[96,3072]{1,0:T(8,128)(2,1)S(1)} collective-permute-done((bf16[96,3072]{1,0:T(8,128)(2,1)S(1)}, bf16[96,3072]{1,0:T(8,128)(2,1)S(1)}, u32[]{:S(2)}, u32[]{:S(2)}) %collective-permute-start.27) | collective-permute-done | bytes 589856 | tf_op jit(solution)/shard_map/ppermute | solution.py:977
  209.6 8.7 %collective-permute-done.26.refs_1_ = bf16[96,3072]{1,0:T(8,128)(2,1)S(1)} collective-permute-done((bf16[96,3072]{1,0:T(8,128)(2,1)S(1)}, bf16[96,3072]{1,0:T(8,128)(2,1)S(1)}, u32[]{:S(2)}, u32[]{:S(2)}) %collective-permute-start.26) | collective-permute-done | bytes 589856 | tf_op jit(solution)/shard_map/ppermute | solution.py:977
  220.6 5.2 %collective-permute-done.28.other_ref = bf16[48,3072]{1,0:T(8,128)(2,1)S(1)} collective-permute-done((bf16[48,3072]{1,0:T(8,128)(2,1)S(1)}, bf16[48,3072]{1,0:T(8,128)(2,1)S(1)}, u32[]{:S(2)}, u32[]{:S(2)}) %collective-permute-start.28) | collective-permute-done | bytes 294944 | tf_op jit(solution)/shard_map/ppermute | solution.py:977
  226.9 19.8 %collective-permute-done.31.other_ref = bf16[192,3072]{1,0:T(8,128)(2,1)S(1)} collective-permute-done((bf16[192,3072]{1,0:T(8,128)(2,1)S(1)}, bf16[192,3072]{1,0:T(8,128)(2,1)S(1)}, u32[]{:S(2)}, u32[]{:S(2)}) %collective-permute-start.31) | collective-permute-done | bytes 1179680 | tf_op jit(solution)/shard_map/ppermute | solution.py:977
  247.4 3.3 %place_turned_half.2.refs_0_ = f32[3072,768]{1,0:T(8,128)} custom-call(s32[12]{0:T(128)S(1)} %stack.60.flag_ref, bf16[384,3072]{1,0:T(8,128)(2,1)S(1)} %join.12.value_ref), custom_call_target="tpu_custom_call" | custom-call | flops 1 | bytes 1 | tf_op jit(solution)/shard_map/place_turned_half/pallas_call | solution.py:951
  255.6 12.5 %collective-permute-done.32.other_ref = bf16[96,3072]{1,0:T(8,128)(2,1)S(1)} collective-permute-done((bf16[96,3072]{1,0:T(8,128)(2,1)S(1)}, bf16[96,3072]{1,0:T(8,128)(2,1)S(1)}, u32[]{:S(2)}, u32[]{:S(2)}) %collective-permute-start.32) | collective-permute-done | bytes 589856 | tf_op jit(solution)/shard_map/ppermute | solution.py:977
  270.8 3.3 %place_turned_half.3 = f32[3072,768]{1,0:T(8,128)} custom-call(s32[12]{0:T(128)S(1)} %stack.60.flag_ref, bf16[384,3072]{1,0:T(8,128)(2,1)S(1)} %collective-permute-done.38.value_ref, f32[3072,768]{1,0:T(8,128)} %place_turned_half.2.refs_0_), custom_call_target="tpu_custom_call", output_to_operand_aliasing={{}: (2, {})} | custom-call | flops 1 | bytes 1 | tf_op jit(solution)/shard_map/place_turned_half/pallas_call | solution.py:951
  274.1 6.2 %collective-permute-done.37.other_ref = bf16[192,3072]{1,0:T(8,128)(2,1)S(1)} collective-permute-done((bf16[192,3072]{1,0:T(8,128)(2,1)S(1)}, bf16[192,3072]{1,0:T(8,128)(2,1)S(1)}, u32[]{:S(2)}, u32[]{:S(2)}) %collective-permute-start.37) | collective-permute-done | bytes 1179680 | tf_op jit(solution)/shard_map/ppermute | solution.py:977
  281.0 2.9 place_half.4.refs_0_
  283.9 9.5 %collective-permute-done.36.other_ref = f32[16,768]{1,0:T(8,128)S(1)} collective-permute-done((f32[16,768]{1,0:T(8,128)S(1)}, f32[16,768]{1,0:T(8,128)S(1)}, u32[]{:S(2)}, u32[]{:S(2)}) %collective-permute-start.36) | collective-permute-done | bytes 49184 | tf_op jit(solution)/shard_map/ppermute | solution.py:971
  297.2 2.9 place_half.6
  300.1 2.9 place_half.7
  (124 shorter events, 48.9 us)
Async XLA Ops:
  25.4 7.9 %collective-permute-start = (bf16[16,896]{1,0:T(8,128)(2,1)S(1)}, bf16[16,896]{1,0:T(8,128)(2,1)S(1)}, u32[]{:S(2)}, u32[]{:S(2)}) collective-permute-start(bf16[16,896]{1,0:T(8,128)(2,1)S(1)} %summarize.1), channel_id=1, source_target_pairs={{0,16},{16,0},{1,17},{17,1},{2,18},{18,2},{3,19},{19,3},{4,20},{20... | collective-permute-start | bytes 86024 | tf_op jit(solution)/shard_map/ppermute | solution.py:971
  33.3 7.6 %collective-permute-start.1 = (bf16[1,2,16,896]{3,2,1,0:T(8,128)(2,1)S(1)}, bf16[1,2,16,896]{3,2,1,0:T(8,128)(2,1)S(1)}, u32[]{:S(2)}, u32[]{:S(2)}) collective-permute-start(bf16[1,2,16,896]{3,2,1,0:T(8,128)(2,1)S(1)} %pad_maximum_fusion.1), channel_id=1, source_target_pairs={{0,8},{1,9},{2,10},{3,11},{4,12},{5,13},{6,14},{7,15},{8,0},{9,1},... | collective-permute-start | bytes 172040 | tf_op jit(solution)/shard_map/ppermute | solution.py:971
  40.9 6.5 %collective-permute-start.2 = (bf16[2,2,16,896]{3,2,1,0:T(8,128)(2,1)S(1)}, bf16[2,2,16,896]{3,2,1,0:T(8,128)(2,1)S(1)}, u32[]{:S(2)}, u32[]{:S(2)}) collective-permute-start(bf16[2,2,16,896]{3,2,1,0:T(8,128)(2,1)S(1)} %constant_dynamic-update-slice_fusion), channel_id=1, source_target_pairs={{0,4},{1,5},{2,6},{3,7},{4,0},{5,1},{6,2},{7,3},{8,12},{9,13},{10,... | collective-permute-start | bytes 344072 | tf_op jit(solution)/shard_map/ppermute | solution.py:971
  47.5 9.2 %collective-permute-start.3 = (bf16[4,2,16,896]{3,2,1,0:T(8,128)(2,1)S(1)}, bf16[4,2,16,896]{3,2,1,0:T(8,128)(2,1)S(1)}, u32[]{:S(2)}, u32[]{:S(2)}) collective-permute-start(bf16[4,2,16,896]{3,2,1,0:T(8,128)(2,1)S(1)} %constant_dynamic-update-slice_fusion.2), channel_id=1, source_target_pairs={{0,2},{1,3},{2,0},{3,1},{4,6},{5,7},{6,4},{7,5},{8,10},{9,11},{10,... | collective-permute-start | bytes 688136 | tf_op jit(solution)/shard_map/ppermute | solution.py:971
  56.8 9.9 %collective-permute-start.4 = (bf16[8,2,16,896]{3,2,1,0:T(8,128)(2,1)S(1)}, bf16[8,2,16,896]{3,2,1,0:T(8,128)(2,1)S(1)}, u32[]{:S(2)}, u32[]{:S(2)}) collective-permute-start(bf16[8,2,16,896]{3,2,1,0:T(8,128)(2,1)S(1)} %constant_dynamic-update-slice_fusion.4), channel_id=1, source_target_pairs={{0,1},{1,0},{2,3},{3,2},{4,5},{5,4},{6,7},{7,6},{8,9},{9,8},{10,11... | collective-permute-start | bytes 1376264 | tf_op jit(solution)/shard_map/ppermute | solution.py:971
  83.1 23.6 %collective-permute-start.13 = (bf16[192,3072]{1,0:T(8,128)(2,1)S(1)}, bf16[192,3072]{1,0:T(8,128)(2,1)S(1)}, u32[]{:S(2)}, u32[]{:S(2)}) collective-permute-start(bf16[192,3072]{1,0:T(8,128)(2,1)S(1)} %get-tuple-element.294), channel_id=1, source_target_pairs={{0,4},{1,3},{2,6},{3,1},{4,0},{5,7},{6,2},{7,5},{8,12},{9,11},{10,... | collective-permute-start | bytes 3538952 | tf_op jit(solution)/shard_map/ppermute | solution.py:977
  107.6 21.2 %collective-permute-start.15 = (bf16[96,3072]{1,0:T(8,128)(2,1)S(1)}, bf16[96,3072]{1,0:T(8,128)(2,1)S(1)}, u32[]{:S(2)}, u32[]{:S(2)}) collective-permute-start(bf16[96,3072]{1,0:T(8,128)(2,1)S(1)} %get-tuple-element.314), channel_id=1, source_target_pairs={{0,8},{1,5},{2,10},{3,7},{4,12},{5,1},{6,14},{7,3},{8,0},{9,13},{1... | collective-permute-start | bytes 1769480 | tf_op jit(solution)/shard_map/ppermute | solution.py:977
  111.5 27.5 %collective-permute-start.14 = (bf16[192,3072]{1,0:T(8,128)(2,1)S(1)}, bf16[192,3072]{1,0:T(8,128)(2,1)S(1)}, u32[]{:S(2)}, u32[]{:S(2)}) collective-permute-start(bf16[192,3072]{1,0:T(8,128)(2,1)S(1)} %get-tuple-element.323), channel_id=1, source_target_pairs={{0,4},{1,3},{2,6},{3,1},{4,0},{5,7},{6,2},{7,5},{8,12},{9,11},{10,... | collective-permute-start | bytes 3538952 | tf_op jit(solution)/shard_map/ppermute | solution.py:977
  129.5 10.4 %collective-permute-start.17 = (bf16[48,3072]{1,0:T(8,128)(2,1)S(1)}, bf16[48,3072]{1,0:T(8,128)(2,1)S(1)}, u32[]{:S(2)}, u32[]{:S(2)}) collective-permute-start(bf16[48,3072]{1,0:T(8,128)(2,1)S(1)} %get-tuple-element.337), channel_id=1, source_target_pairs={{0,2},{1,9},{2,0},{3,11},{4,6},{5,13},{6,4},{7,15},{8,10},{9,1},{1... | collective-permute-start | bytes 884744 | tf_op jit(solution)/shard_map/ppermute | solution.py:977
  135.1 10.8 %collective-permute-start.18 = (bf16[384,768]{1,0:T(8,128)(2,1)S(1)}, bf16[384,768]{1,0:T(8,128)(2,1)S(1)}, u32[]{:S(2)}, u32[]{:S(2)}) collective-permute-start(bf16[384,768]{1,0:T(8,128)(2,1)S(1)} %get-tuple-element.341), channel_id=1, source_target_pairs={{0,1},{1,0},{2,3},{3,2},{4,5},{5,4},{6,7},{7,6},{8,9},{9,8},{10,11... | collective-permute-start | bytes 1769480 | tf_op jit(solution)/shard_map/ppermute | solution.py:971
  135.1 10.9 %collective-permute-start.19 = (bf16[384,768]{1,0:T(8,128)(2,1)S(1)}, bf16[384,768]{1,0:T(8,128)(2,1)S(1)}, u32[]{:S(2)}, u32[]{:S(2)}) collective-permute-start(bf16[384,768]{1,0:T(8,128)(2,1)S(1)} %get-tuple-element.363), channel_id=1, source_target_pairs={{0,1},{1,0},{2,3},{3,2},{4,5},{5,4},{6,7},{7,6},{8,9},{9,8},{10,11... | collective-permute-start | bytes 1769480 | tf_op jit(solution)/shard_map/ppermute | solution.py:971
  135.6 10.9 %collective-permute-start.20 = (bf16[384,768]{1,0:T(8,128)(2,1)S(1)}, bf16[384,768]{1,0:T(8,128)(2,1)S(1)}, u32[]{:S(2)}, u32[]{:S(2)}) collective-permute-start(bf16[384,768]{1,0:T(8,128)(2,1)S(1)} %get-tuple-element.364), channel_id=1, source_target_pairs={{0,1},{1,0},{2,3},{3,2},{4,5},{5,4},{6,7},{7,6},{8,9},{9,8},{10,11... | collective-permute-start | bytes 1769480 | tf_op jit(solution)/shard_map/ppermute | solution.py:971
  139.0 7.6 %collective-permute-start.21 = (bf16[384,768]{1,0:T(8,128)(2,1)S(1)}, bf16[384,768]{1,0:T(8,128)(2,1)S(1)}, u32[]{:S(2)}, u32[]{:S(2)}) collective-permute-start(bf16[384,768]{1,0:T(8,128)(2,1)S(1)} %get-tuple-element.365), channel_id=1, source_target_pairs={{0,1},{1,0},{2,3},{3,2},{4,5},{5,4},{6,7},{7,6},{8,9},{9,8},{10,11... | collective-permute-start | bytes 1769480 | tf_op jit(solution)/shard_map/ppermute | solution.py:971
  139.9 26.7 %collective-permute-start.16 = (bf16[96,3072]{1,0:T(8,128)(2,1)S(1)}, bf16[96,3072]{1,0:T(8,128)(2,1)S(1)}, u32[]{:S(2)}, u32[]{:S(2)}) collective-permute-start(bf16[96,3072]{1,0:T(8,128)(2,1)S(1)} %get-tuple-element.345), channel_id=1, source_target_pairs={{0,8},{1,5},{2,10},{3,7},{4,12},{5,1},{6,14},{7,3},{8,0},{9,13},{1... | collective-permute-start | bytes 1769480 | tf_op jit(solution)/shard_map/ppermute | solution.py:977
  145.9 29.5 %collective-permute-start.24 = (bf16[48,3072]{1,0:T(8,128)(2,1)S(1)}, bf16[48,3072]{1,0:T(8,128)(2,1)S(1)}, u32[]{:S(2)}, u32[]{:S(2)}) collective-permute-start(bf16[48,3072]{1,0:T(8,128)(2,1)S(1)} %add.83.mine_ref), channel_id=1, source_target_pairs={{0,2},{1,9},{2,0},{3,11},{4,6},{5,13},{6,4},{7,15},{8,10},{9,1},{1... | collective-permute-start | bytes 884744 | tf_op jit(solution)/shard_map/ppermute | solution.py:977
  146.0 29.4 %collective-permute-start.25 = (f32[16,768]{1,0:T(8,128)S(1)}, f32[16,768]{1,0:T(8,128)S(1)}, u32[]{:S(2)}, u32[]{:S(2)}) collective-permute-start(f32[16,768]{1,0:T(8,128)S(1)} %pack_vectors.1.mine_ref), channel_id=1, source_target_pairs={{0,1},{1,0},{2,3},{3,2},{4,5},{5,4},{6,7},{7,6},{8,9},{9,8},{10,11... | collective-permute-start | bytes 147464 | tf_op jit(solution)/shard_map/ppermute | solution.py:971
  147.8 31.6 %collective-permute-start.22 = (bf16[192,3072]{1,0:T(8,128)(2,1)S(1)}, bf16[192,3072]{1,0:T(8,128)(2,1)S(1)}, u32[]{:S(2)}, u32[]{:S(2)}) collective-permute-start(bf16[192,3072]{1,0:T(8,128)(2,1)S(1)} %get-tuple-element.374), channel_id=1, source_target_pairs={{0,4},{1,3},{2,6},{3,1},{4,0},{5,7},{6,2},{7,5},{8,12},{9,11},{10,... | collective-permute-start | bytes 3538952 | tf_op jit(solution)/shard_map/ppermute | solution.py:977
  167.3 8.8 %collective-permute-start.23 = (bf16[48,3072]{1,0:T(8,128)(2,1)S(1)}, bf16[48,3072]{1,0:T(8,128)(2,1)S(1)}, u32[]{:S(2)}, u32[]{:S(2)}) collective-permute-start(bf16[48,3072]{1,0:T(8,128)(2,1)S(1)} %get-tuple-element.377), channel_id=1, source_target_pairs={{0,2},{1,9},{2,0},{3,11},{4,6},{5,13},{6,4},{7,15},{8,10},{9,1},{1... | collective-permute-start | bytes 884744 | tf_op jit(solution)/shard_map/ppermute | solution.py:977
  176.0 32.1 %collective-permute-start.27 = (bf16[96,3072]{1,0:T(8,128)(2,1)S(1)}, bf16[96,3072]{1,0:T(8,128)(2,1)S(1)}, u32[]{:S(2)}, u32[]{:S(2)}) collective-permute-start(bf16[96,3072]{1,0:T(8,128)(2,1)S(1)} %join.9.mine_ref), channel_id=1, source_target_pairs={{0,8},{1,5},{2,10},{3,7},{4,12},{5,1},{6,14},{7,3},{8,0},{9,13},{1... | collective-permute-start | bytes 1769480 | tf_op jit(solution)/shard_map/ppermute | solution.py:977
  180.4 37.9 %collective-permute-start.26 = (bf16[96,3072]{1,0:T(8,128)(2,1)S(1)}, bf16[96,3072]{1,0:T(8,128)(2,1)S(1)}, u32[]{:S(2)}, u32[]{:S(2)}) collective-permute-start(bf16[96,3072]{1,0:T(8,128)(2,1)S(1)} %get-tuple-element.391), channel_id=1, source_target_pairs={{0,8},{1,5},{2,10},{3,7},{4,12},{5,1},{6,14},{7,3},{8,0},{9,13},{1... | collective-permute-start | bytes 1769480 | tf_op jit(solution)/shard_map/ppermute | solution.py:977
  208.7 37.9 %collective-permute-start.31 = (bf16[192,3072]{1,0:T(8,128)(2,1)S(1)}, bf16[192,3072]{1,0:T(8,128)(2,1)S(1)}, u32[]{:S(2)}, u32[]{:S(2)}) collective-permute-start(bf16[192,3072]{1,0:T(8,128)(2,1)S(1)} %join.10.mine_ref), channel_id=1, source_target_pairs={{0,4},{1,3},{2,6},{3,1},{4,0},{5,7},{6,2},{7,5},{8,12},{9,11},{10,... | collective-permute-start | bytes 3538952 | tf_op jit(solution)/shard_map/ppermute | solution.py:977
  208.8 11.2 %collective-permute-start.29 = (bf16[48,3072]{1,0:T(8,128)(2,1)S(1)}, bf16[48,3072]{1,0:T(8,128)(2,1)S(1)}, u32[]{:S(2)}, u32[]{:S(2)}) collective-permute-start(bf16[48,3072]{1,0:T(8,128)(2,1)S(1)} %add.85.mine_ref), channel_id=1, source_target_pairs={{0,2},{1,9},{2,0},{3,11},{4,6},{5,13},{6,4},{7,15},{8,10},{9,1},{1... | collective-permute-start | bytes 884744 | tf_op jit(solution)/shard_map/ppermute | solution.py:977
  219.0 6.8 %collective-permute-start.28 = (bf16[48,3072]{1,0:T(8,128)(2,1)S(1)}, bf16[48,3072]{1,0:T(8,128)(2,1)S(1)}, u32[]{:S(2)}, u32[]{:S(2)}) collective-permute-start(bf16[48,3072]{1,0:T(8,128)(2,1)S(1)} %get-tuple-element.397), channel_id=1, source_target_pairs={{0,2},{1,9},{2,0},{3,11},{4,6},{5,13},{6,4},{7,15},{8,10},{9,1},{1... | collective-permute-start | bytes 884744 | tf_op jit(solution)/shard_map/ppermute | solution.py:977
  225.9 24.8 %collective-permute-start.30 = (bf16[48,3072]{1,0:T(8,128)(2,1)S(1)}, bf16[48,3072]{1,0:T(8,128)(2,1)S(1)}, u32[]{:S(2)}, u32[]{:S(2)}) collective-permute-start(bf16[48,3072]{1,0:T(8,128)(2,1)S(1)} %add.86.mine_ref), channel_id=1, source_target_pairs={{0,2},{1,9},{2,0},{3,11},{4,6},{5,13},{6,4},{7,15},{8,10},{9,1},{1... | collective-permute-start | bytes 884744 | tf_op jit(solution)/shard_map/ppermute | solution.py:977
  226.9 25.5 %collective-permute-start.34 = (bf16[96,3072]{1,0:T(8,128)(2,1)S(1)}, bf16[96,3072]{1,0:T(8,128)(2,1)S(1)}, u32[]{:S(2)}, u32[]{:S(2)}) collective-permute-start(bf16[96,3072]{1,0:T(8,128)(2,1)S(1)} %join.11.mine_ref), channel_id=1, source_target_pairs={{0,8},{1,5},{2,10},{3,7},{4,12},{5,1},{6,14},{7,3},{8,0},{9,13},{1... | collective-permute-start | bytes 1769480 | tf_op jit(solution)/shard_map/ppermute | solution.py:977
  247.3 23.4 %collective-permute-start.38 = (bf16[384,3072]{1,0:T(8,128)(2,1)S(1)}, bf16[384,3072]{1,0:T(8,128)(2,1)S(1)}, u32[]{:S(2)}, u32[]{:S(2)}) collective-permute-start(bf16[384,3072]{1,0:T(8,128)(2,1)S(1)} %join.12.value_ref), channel_id=1, source_target_pairs={{0,1},{1,0},{2,3},{3,2},{4,5},{5,4},{6,7},{7,6},{8,9},{9,8},{10,11... | collective-permute-start | bytes 7077896 | tf_op jit(solution)/shard_map/ppermute | solution.py:971
  251.3 16.8 %collective-permute-start.32 = (bf16[96,3072]{1,0:T(8,128)(2,1)S(1)}, bf16[96,3072]{1,0:T(8,128)(2,1)S(1)}, u32[]{:S(2)}, u32[]{:S(2)}) collective-permute-start(bf16[96,3072]{1,0:T(8,128)(2,1)S(1)} %join.13.mine_ref), channel_id=1, source_target_pairs={{0,8},{1,5},{2,10},{3,7},{4,12},{5,1},{6,14},{7,3},{8,0},{9,13},{1... | collective-permute-start | bytes 1769480 | tf_op jit(solution)/shard_map/ppermute | solution.py:977
  253.0 27.3 %collective-permute-start.37 = (bf16[192,3072]{1,0:T(8,128)(2,1)S(1)}, bf16[192,3072]{1,0:T(8,128)(2,1)S(1)}, u32[]{:S(2)}, u32[]{:S(2)}) collective-permute-start(bf16[192,3072]{1,0:T(8,128)(2,1)S(1)} %join.14.mine_ref), channel_id=1, source_target_pairs={{0,4},{1,3},{2,6},{3,1},{4,0},{5,7},{6,2},{7,5},{8,12},{9,11},{10,... | collective-permute-start | bytes 3538952 | tf_op jit(solution)/shard_map/ppermute | solution.py:977
  268.7 24.8 %collective-permute-start.35 = (bf16[192,3072]{1,0:T(8,128)(2,1)S(1)}, bf16[192,3072]{1,0:T(8,128)(2,1)S(1)}, u32[]{:S(2)}, u32[]{:S(2)}) collective-permute-start(bf16[192,3072]{1,0:T(8,128)(2,1)S(1)} %join.15.mine_ref), channel_id=1, source_target_pairs={{0,4},{1,3},{2,6},{3,1},{4,0},{5,7},{6,2},{7,5},{8,12},{9,11},{10,... | collective-permute-start | bytes 3538952 | tf_op jit(solution)/shard_map/ppermute | solution.py:977
  268.8 24.7 %collective-permute-start.36 = (f32[16,768]{1,0:T(8,128)S(1)}, f32[16,768]{1,0:T(8,128)S(1)}, u32[]{:S(2)}, u32[]{:S(2)}) collective-permute-start(f32[16,768]{1,0:T(8,128)S(1)} %add.87.mine_ref), channel_id=1, source_target_pairs={{0,4},{1,5},{2,6},{3,7},{4,0},{5,1},{6,2},{7,3},{8,12},{9,13},{10,... | collective-permute-start | bytes 147464 | tf_op jit(solution)/shard_map/ppermute | solution.py:971
  281.0 16.3 %collective-permute-start.40 = (bf16[384,3072]{1,0:T(8,128)(2,1)S(1)}, bf16[384,3072]{1,0:T(8,128)(2,1)S(1)}, u32[]{:S(2)}, u32[]{:S(2)}) collective-permute-start(bf16[384,3072]{1,0:T(8,128)(2,1)S(1)} %join.16.value_ref), channel_id=1, source_target_pairs={{0,1},{1,0},{2,3},{3,2},{4,5},{5,4},{6,7},{7,6},{8,9},{9,8},{10,11... | collective-permute-start | bytes 7077896 | tf_op jit(solution)/shard_map/ppermute | solution.py:971
  294.2 8.8 %collective-permute-start.41 = (f32[16,768]{1,0:T(8,128)S(1)}, f32[16,768]{1,0:T(8,128)S(1)}, u32[]{:S(2)}, u32[]{:S(2)}) collective-permute-start(f32[16,768]{1,0:T(8,128)S(1)} %add.88.mine_ref), channel_id=1, source_target_pairs={{0,8},{1,9},{2,10},{3,11},{4,12},{5,13},{6,14},{7,15},{8,0},{9,1},... | collective-permute-start | bytes 147464 | tf_op jit(solution)/shard_map/ppermute | solution.py:971
  (16 other events, 105.5 us)
where the time goes:
time: 304 us
  Pallas kernels  155 us (51%)
  waiting for transfers between devices  111 us (37%)
  starting transfers between devices  31.6 us (10%)
  local copies, waits for them, and re-layouts  3.55 us (1%)
    ppermute x18, waiting for transfers between devices, swapped_by_core(): return lax.ppermute(value, 'batch', pairs)  98.3 us
    pallas_call x1, Pallas kernels, feed_back(): pl.pallas_call(feed_kernel, grid_spec=pltpu.PrefetchScalarGridSpec(num_sc...  21.4 us
    pallas_call x4, Pallas kernels, widen(): pl.pallas_call(widen_kernel, grid=(steps,), in_specs=[whole(low.shape), c...  19.6 us
    pallas_call x1, Pallas kernels, attend(): pl.pallas_call(attend_kernel, grid_spec=pltpu.PrefetchScalarGridSpec(num_...  17.6 us
    pallas_call x1, Pallas kernels, attend_back(): pl.pallas_call(attend_back_kernel, grid=(count // ROWS,), in_specs=[row_b...  16.2 us
    ppermute x18, starting transfers between devices, swapped_by_core(): return lax.ppermute(value, 'batch', pairs)  15.9 us
    ppermute x24, starting transfers between devices, swapped(): return lax.ppermute(value, axis, pairs)  15.7 us
    ppermute x24, waiting for transfers between devices, swapped(): return lax.ppermute(value, axis, pairs)  12.8 us
  transfers between devices with their start and end apart: 42, of which 14 were waited for; matrix products, arithmetic and copies ran while one was open for 0% of the time, Pallas kernels for 40%

commit v1 on v0

--- a/solution.py
+++ b/solution.py
@@ -383,7 +383,7 @@
             jax.ShapeDtypeStruct((count, width), BRAIN),
         ],
         cost_estimate=cost(1, 1),
-        compiler_params=pltpu.CompilerParams(vmem_limit_bytes=14 * MEGA),
+        compiler_params=pltpu.CompilerParams(vmem_limit_bytes=8 * MEGA),
         name="shrink",
     )(active, shrink, normal, *first, settle, *second)
 
@@ -1152,7 +1152,7 @@
         elif part == parts:
             active, slope = wide_pair
             normal_two, inverse_two, encoded = run(
-                lambda a, n: shrink_back_to_width(a, shrink, n, first, settling, second),
+                lambda a, n: shrink_back_to_width(a, contraction[0], n, first, settling, second),
                 active,
                 normal_one,
             )

time: 304 us -> 288 us (0.947)
  waiting for transfers between devices: 111 us -> 97.3 us
    ppermute x18, waiting for transfers between devices: 98.3 us -> 85.8 us  [swapped_by_core(): return lax.ppermute(value, 'batch', pairs)]
  transfers between devices with their start and end apart: 42 -> 42, of which waited for: 14 -> 13; matrix products, arithmetic and copies ran while one was open for 0% -> 0% of each run, Pallas kernels for 40% -> 41%
where the time goes in v1:
time: 288 us
  Pallas kernels  154 us (53%)
  waiting for transfers between devices  97.3 us (34%)
  starting transfers between devices  29 us (10%)
  local copies, waits for them, and re-layouts  5.44 us (2%)
    ppermute x18, waiting for transfers between devices, swapped_by_core(): return lax.ppermute(value, 'batch', pairs)  85.8 us
    pallas_call x1, Pallas kernels, feed_back(): pl.pallas_call(feed_kernel, grid_spec=pltpu.PrefetchScalarGridSpec(num_sc...  21.2 us
    pallas_call x4, Pallas kernels, widen(): pl.pallas_call(widen_kernel, grid=(steps,), in_specs=[whole(low.shape), c...  19.7 us
    pallas_call x1, Pallas kernels, attend(): pl.pallas_call(attend_kernel, grid_spec=pltpu.PrefetchScalarGridSpec(num_...  17.7 us
    pallas_call x1, Pallas kernels, attend_back(): pl.pallas_call(attend_back_kernel, grid=(count // ROWS,), in_specs=[row_b...  16.2 us
    ppermute x24, starting transfers between devices, swapped(): return lax.ppermute(value, axis, pairs)  15.9 us
    ppermute x18, starting transfers between devices, swapped_by_core(): return lax.ppermute(value, 'batch', pairs)  13.1 us
    pallas_call x4, Pallas kernels, place_half(): pl.pallas_call(functools.partial(place_kernel, kept=len(kept)), grid_spec...  11.5 us
  transfers between devices with their start and end apart: 42, of which 13 were waited for; matrix products, arithmetic and copies ran while one was open for 0% of the time, Pallas kernels for 41%

profile of v1, /device:TPU:0, one launch (start us, length us, event | category | flops | bytes accessed | tf_op | source)
XLA Modules:
  0.0 287.8 jit_solution(493871929214957533)
XLA Ops:
  1.9 17.7 %attend.1 = (bf16[1024,2304]{1,0:T(8,128)(2,1)S(1)}, bf16[4,6,256,512]{3,2,1,0:T(8,128)(2,1)S(1)}, bf16[1024,768]{1,0:T(8,128)(2,1)S(1)}, f32[1024,768]{1,0:T(8,...) custom-call(s32[12]{0:T(128)S(1)} %stack.60.flag_ref, bf16[1024,768]{1,0:T(8,128)(2,1)} %bitcast.51, ...), custom_call_target="tpu_custom_call" | custom-call | flops 1 | bytes 1 | tf_op jit(solution)/shard_map/attend/pallas_call | solution.py:173
  19.6 5.9 %summarize.1 = bf16[16,896]{1,0:T(8,128)(2,1)S(1)} custom-call(s32[12]{0:T(128)S(1)} %stack.60.flag_ref, s32[16]{0:T(128)S(1)} %copy-done.4, s32[16]{0:T(128)S(1)} %copy-done.5, f32[128,8,768]{2,1,0:T(8,128)S(1)} %bitcast.41, bf16[1,768]{1,0:T(2,128)(2,1)} %gain_ref.5, bf16[1,768]{1,0:T(2,128)(2,1)} %shift_one_ref.3, bf16[768,3072]{1,0:T(8,128)(2,1)S(1)} %bitcast.30, ...), custom_call_target="tpu_custom_call" | custom-call | flops 1 | bytes 1 | tf_op jit(solution)/shard_map/summarize/pallas_call | solution.py:275
  25.5 3.0 %collective-permute-start = (bf16[16,896]{1,0:T(8,128)(2,1)S(1)}, bf16[16,896]{1,0:T(8,128)(2,1)S(1)}, u32[]{:S(2)}, u32[]{:S(2)}) collective-permute-start(bf16[16,896]{1,0:T(8,128)(2,1)S(1)} %summarize.1), channel_id=1, source_target_pairs={{0,16},{16,0},{1,17},{17,1},{2,18},{18,2},{3,19},{19,3},{4,20},{20... | collective-permute-start | bytes 86024 | tf_op jit(solution)/shard_map/ppermute | solution.py:971
  28.5 4.9 %widen.4 = (bf16[1024,3072]{1,0:T(8,128)(2,1)S(1)}, bf16[1024,3072]{1,0:T(8,128)(2,1)S(1)}) custom-call(bf16[1024,768]{1,0:T(8,128)(2,1)S(1)} %get-tuple-element.251.low_ref, bf16[768,3072]{1,0:T(8,128)(2,1)S(1)} %bitcast.31, bf16[1,3072]{1,0:T(2,128)(2,1)} %lift_ref.9), custom_call_target="tpu_custom_call" | custom-call | flops 1 | bytes 1 | tf_op jit(solution)/shard_map/widen/pallas_call | solution.py:336
  36.1 4.9 %widen.5 = (bf16[1024,3072]{1,0:T(8,128)(2,1)S(1)}, bf16[1024,3072]{1,0:T(8,128)(2,1)S(1)}) custom-call(bf16[1024,768]{1,0:T(8,128)(2,1)S(1)} %get-tuple-element.251.low_ref, bf16[768,3072]{1,0:T(8,128)(2,1)S(1)} %bitcast.32, bf16[1,3072]{1,0:T(2,128)(2,1)} %lift_ref.9, ...), custom_call_target="tpu_custom_call", output_to_operand_aliasing={{0}: (3, {}), {1}: (4, {})} | custom-call | flops 1 | bytes 1 | tf_op jit(solution)/shard_map/widen/pallas_call | solution.py:336
  42.7 4.9 %widen.6 = (bf16[1024,3072]{1,0:T(8,128)(2,1)S(1)}, bf16[1024,3072]{1,0:T(8,128)(2,1)S(1)}) custom-call(bf16[1024,768]{1,0:T(8,128)(2,1)S(1)} %get-tuple-element.251.low_ref, bf16[768,3072]{1,0:T(8,128)(2,1)S(1)} %bitcast.33, bf16[1,3072]{1,0:T(2,128)(2,1)} %lift_ref.9, ...), custom_call_target="tpu_custom_call", output_to_operand_aliasing={{0}: (3, {}), {1}: (4, {})} | custom-call | flops 1 | bytes 1 | tf_op jit(solution)/shard_map/widen/pallas_call | solution.py:336
  49.2 5.0 %widen.7 = (bf16[1024,3072]{1,0:T(8,128)(2,1)S(1)}, bf16[1024,3072]{1,0:T(8,128)(2,1)S(1)}) custom-call(bf16[1024,768]{1,0:T(8,128)(2,1)S(1)} %get-tuple-element.251.low_ref, bf16[768,3072]{1,0:T(8,128)(2,1)S(1)} %bitcast.34, bf16[1,3072]{1,0:T(2,128)(2,1)} %lift_ref.9, ...), custom_call_target="tpu_custom_call", output_to_operand_aliasing={{0}: (3, {}), {1}: (4, {})} | custom-call | flops 1 | bytes 1 | tf_op jit(solution)/shard_map/widen/pallas_call | solution.py:336
  54.3 2.7 copy-done.2
  57.1 8.3 %shrink.1 = (f32[1024,768]{1,0:T(8,128)S(1)}, f32[1024,1]{1,0:T(8,128)S(1)}, bf16[1024,768]{1,0:T(8,128)(2,1)}) custom-call(bf16[1024,3072]{1,0:T(8,128)(2,1)S(1)} %get-tuple-element.278.active_ref, bf16[3072,768]{1,0:T(8,128)(2,1)S(1)} %bitcast.40, f32[1024,768]{1,0:T(8,128)S(1)} %get-tuple-element.325.normal_ref, bf16[1,768]{1,0:T(2,128)(2,1)} %gain_ref.5, ...), custom_call_target="tpu_custom_call" | custom-call | flops 1 | bytes 1 | tf_op jit(solution)/shard_map/shrink/pallas_call | solution.py:375
  65.5 5.5 %contrast.1 = (f32[1024,768]{1,0:T(8,128)S(1)}, bf16[1024,768]{1,0:T(8,128)(2,1)S(1)}, f32[8,768]{1,0:T(8,128)S(1)}) custom-call(s32[12]{0:T(128)S(1)} %stack.60.flag_ref, s32[16]{0:T(128)S(1)} %copy-done.4, bf16[16,2,16,896]{3,2,1,0:T(8,128)(2,1)S(1)} %pad_maximum_fusion.every_ref, s32[1,256]{1,0:T(1,128)S(1)} %select_n.48.column_ref, ...), custom_call_target="tpu_custom_call" | custom-call | flops 1 | bytes 1 | tf_op jit(solution)/shard_map/contrast/pallas_call | solution.py:490
  71.0 4.2 %contraction_half.2 = (bf16[384,768]{1,0:T(8,128)(2,1)S(1)}, bf16[384,768]{1,0:T(8,128)(2,1)S(1)}, bf16[384,768]{1,0:T(8,128)(2,1)S(1)}, bf16[384,768]{1,0:T(8,128)(2,1)S(1)}) custom-call(s32[1]{0:T(128)S(6)} %sub.7.flag_ref, bf16[1024,768]{1,0:T(8,128)(2,1)S(1)} %get-tuple-element.295.low_ref.two_low_ref, bf16[1024,3072]{1,0:T(8,128)(2,1)S(1)} %get-tuple-element.278.active_ref), custom_call_target="tpu_custom_call" | custom-call | flops 99999997952 | bytes 1 | tf_op jit(solution)/shard_map/contraction_half/pallas_call | solution.py:541
  76.3 4.2 %contraction_half.3 = (bf16[384,768]{1,0:T(8,128)(2,1)S(1)}, bf16[384,768]{1,0:T(8,128)(2,1)S(1)}, bf16[384,768]{1,0:T(8,128)(2,1)S(1)}, bf16[384,768]{1,0:T(8,128)(2,1)S(1)}) custom-call(s32[1]{0:T(128)} %bitcast.1.flag_ref, bf16[1024,768]{1,0:T(8,128)(2,1)S(1)} %get-tuple-element.295.low_ref.two_low_ref, bf16[1024,3072]{1,0:T(8,128)(2,1)S(1)} %get-tuple-element.278.active_ref), custom_call_target="tpu_custom_call" | custom-call | flops 99999997952 | bytes 1 | tf_op jit(solution)/shard_map/contraction_half/pallas_call | solution.py:541
  82.9 21.2 %feed_back.1 = (f32[1,3072]{1,0:T(1,128)S(1)}, f32[1024,768]{1,0:T(8,128)S(1)}, bf16[384,768]{1,0:T(8,128)(2,1)S(1)}, bf16[384,768]{1,0:T(8,128)(2,1)S(1)}, bf16...) custom-call(s32[12]{0:T(128)S(1)} %stack.60.flag_ref, ...), custom_call_target="tpu_custom_call" | custom-call | flops 6000000000 | bytes 1 | tf_op jit(solution)/shard_map/feed_back/pallas_call | solution.py:605
  113.0 16.2 %attend_back.1 = (f32[1024,768]{1,0:T(8,128)S(1)}, bf16[1024,768]{1,0:T(8,128)(2,1)S(1)}, bf16[1024,2304]{1,0:T(8,128)(2,1)S(1)}, f32[8,768]{1,0:T(8,128)S(1)}, f32[1,2304]{1,0:T(1,128)S(1)}) custom-call(f32[1024,768]{1,0:T(8,128)S(1)} %copy-done.7, f32[1024,768]{1,0:T(8,128)S(1)} %get-tuple-element.325.normal_ref, ...), custom_call_target="tpu_custom_call" | custom-call | flops 6000000000 | bytes 1 | tf_op jit(solution)/shard_map/attend_back/pallas_call | solution.py:691
  130.6 5.0 %merge_project_half.2 = (bf16[384,768]{1,0:T(8,128)(2,1)S(1)}, bf16[384,768]{1,0:T(8,128)(2,1)S(1)}, bf16[384,768]{1,0:T(8,128)(2,1)S(1)}, bf16[384,768]{1,0:T(8,128)(2,1)S(1)}) custom-call(s32[1]{0:T(128)S(6)} %sub.7.flag_ref, bf16[1024,768]{1,0:T(8,128)(2,1)S(1)} %get-tuple-element.356.context_ref, bf16[1024,768]{1,0:T(8,128)(2,1)S(1)} %get-tuple-element.357.one_ref, ...), custom_call_target="tpu_custom_call" | custom-call | flops 20000000000 | bytes 1 | tf_op jit(solution)/shard_map/merge_project_half/pallas_call | solution.py:747
  139.3 5.0 %merge_project_half.3 = (bf16[384,768]{1,0:T(8,128)(2,1)S(1)}, bf16[384,768]{1,0:T(8,128)(2,1)S(1)}, bf16[384,768]{1,0:T(8,128)(2,1)S(1)}, bf16[384,768]{1,0:T(8,128)(2,1)S(1)}) custom-call(s32[1]{0:T(128)} %bitcast.1.flag_ref, bf16[1024,768]{1,0:T(8,128)(2,1)S(1)} %get-tuple-element.356.context_ref, bf16[1024,768]{1,0:T(8,128)(2,1)S(1)} %get-tuple-element.357.one_ref, ...), custom_call_target="tpu_custom_call" | custom-call | flops 20000000000 | bytes 1 | tf_op jit(solution)/shard_map/merge_project_half/pallas_call | solution.py:747
  147.9 12.9 %collective-permute-done.16.refs_1_ = bf16[96,3072]{1,0:T(8,128)(2,1)S(1)} collective-permute-done((bf16[96,3072]{1,0:T(8,128)(2,1)S(1)}, bf16[96,3072]{1,0:T(8,128)(2,1)S(1)}, u32[]{:S(2)}, u32[]{:S(2)}) %collective-permute-start.16) | collective-permute-done | bytes 589856 | tf_op jit(solution)/shard_map/ppermute | solution.py:977
  164.2 7.4 %tokens_back.1 = f32[1024,768]{1,0:T(8,128)} custom-call(f32[1024,768]{1,0:T(8,128)S(1)} %get-tuple-element.378.one_ref, bf16[1024,2304]{1,0:T(8,128)(2,1)S(1)} %get-tuple-element.379.packed_ref, bf16[768,2304]{1,0:T(8,128)(2,1)} %bitcast.46), custom_call_target="tpu_custom_call" | custom-call | flops 1 | bytes 1 | tf_op jit(solution)/shard_map/tokens_back/pallas_call | solution.py:851
  172.4 6.5 %collective-permute-done.22.refs_1_ = bf16[192,3072]{1,0:T(8,128)(2,1)S(1)} collective-permute-done((bf16[192,3072]{1,0:T(8,128)(2,1)S(1)}, bf16[192,3072]{1,0:T(8,128)(2,1)S(1)}, u32[]{:S(2)}, u32[]{:S(2)}) %collective-permute-start.22) | collective-permute-done | bytes 1179680 | tf_op jit(solution)/shard_map/ppermute | solution.py:977
  179.9 9.5 %collective-permute-done.27.other_ref = bf16[96,3072]{1,0:T(8,128)(2,1)S(1)} collective-permute-done((bf16[96,3072]{1,0:T(8,128)(2,1)S(1)}, bf16[96,3072]{1,0:T(8,128)(2,1)S(1)}, u32[]{:S(2)}, u32[]{:S(2)}) %collective-permute-start.27) | collective-permute-done | bytes 589856 | tf_op jit(solution)/shard_map/ppermute | solution.py:977
  191.0 22.4 %collective-permute-done.26.refs_1_ = bf16[96,3072]{1,0:T(8,128)(2,1)S(1)} collective-permute-done((bf16[96,3072]{1,0:T(8,128)(2,1)S(1)}, bf16[96,3072]{1,0:T(8,128)(2,1)S(1)}, u32[]{:S(2)}, u32[]{:S(2)}) %collective-permute-start.26) | collective-permute-done | bytes 589856 | tf_op jit(solution)/shard_map/ppermute | solution.py:977
  215.4 5.5 %collective-permute-done.28.other_ref = bf16[48,3072]{1,0:T(8,128)(2,1)S(1)} collective-permute-done((bf16[48,3072]{1,0:T(8,128)(2,1)S(1)}, bf16[48,3072]{1,0:T(8,128)(2,1)S(1)}, u32[]{:S(2)}, u32[]{:S(2)}) %collective-permute-start.28) | collective-permute-done | bytes 294944 | tf_op jit(solution)/shard_map/ppermute | solution.py:977
  222.5 3.3 %place_turned_half.2.refs_0_ = f32[3072,768]{1,0:T(8,128)} custom-call(s32[12]{0:T(128)S(1)} %stack.60.flag_ref, bf16[384,3072]{1,0:T(8,128)(2,1)S(1)} %join.12.value_ref), custom_call_target="tpu_custom_call" | custom-call | flops 1 | bytes 1 | tf_op jit(solution)/shard_map/place_turned_half/pallas_call | solution.py:951
  230.8 11.6 %collective-permute-done.34.other_ref = bf16[96,3072]{1,0:T(8,128)(2,1)S(1)} collective-permute-done((bf16[96,3072]{1,0:T(8,128)(2,1)S(1)}, bf16[96,3072]{1,0:T(8,128)(2,1)S(1)}, u32[]{:S(2)}, u32[]{:S(2)}) %collective-permute-start.34) | collective-permute-done | bytes 589856 | tf_op jit(solution)/shard_map/ppermute | solution.py:977
  243.1 8.3 %collective-permute-done.32.other_ref = bf16[96,3072]{1,0:T(8,128)(2,1)S(1)} collective-permute-done((bf16[96,3072]{1,0:T(8,128)(2,1)S(1)}, bf16[96,3072]{1,0:T(8,128)(2,1)S(1)}, u32[]{:S(2)}, u32[]{:S(2)}) %collective-permute-start.32) | collective-permute-done | bytes 589856 | tf_op jit(solution)/shard_map/ppermute | solution.py:977
  254.2 3.3 %place_turned_half.3 = f32[3072,768]{1,0:T(8,128)} custom-call(s32[12]{0:T(128)S(1)} %stack.60.flag_ref, bf16[384,3072]{1,0:T(8,128)(2,1)S(1)} %collective-permute-done.38.value_ref, f32[3072,768]{1,0:T(8,128)} %place_turned_half.2.refs_0_), custom_call_target="tpu_custom_call", output_to_operand_aliasing={{}: (2, {})} | custom-call | flops 1 | bytes 1 | tf_op jit(solution)/shard_map/place_turned_half/pallas_call | solution.py:951
  257.4 7.1 %collective-permute-done.37.other_ref = bf16[192,3072]{1,0:T(8,128)(2,1)S(1)} collective-permute-done((bf16[192,3072]{1,0:T(8,128)(2,1)S(1)}, bf16[192,3072]{1,0:T(8,128)(2,1)S(1)}, u32[]{:S(2)}, u32[]{:S(2)}) %collective-permute-start.37) | collective-permute-done | bytes 1179680 | tf_op jit(solution)/shard_map/ppermute | solution.py:977
  265.3 2.9 %place_half.4.refs_0_ = f32[768,3072]{1,0:T(8,128)} custom-call(s32[12]{0:T(128)S(1)} %stack.60.flag_ref, bf16[384,3072]{1,0:T(8,128)(2,1)S(1)} %join.16.value_ref), custom_call_target="tpu_custom_call" | custom-call | flops 1 | bytes 1 | tf_op jit(solution)/shard_map/place_half/pallas_call | solution.py:924
  268.2 9.5 %collective-permute-done.36.other_ref = f32[16,768]{1,0:T(8,128)S(1)} collective-permute-done((f32[16,768]{1,0:T(8,128)S(1)}, f32[16,768]{1,0:T(8,128)S(1)}, u32[]{:S(2)}, u32[]{:S(2)}) %collective-permute-start.36) | collective-permute-done | bytes 49184 | tf_op jit(solution)/shard_map/ppermute | solution.py:971
  278.5 2.9 place_half.5
  281.4 2.9 %place_half.6 = f32[768,3072]{1,0:T(8,128)} custom-call(s32[12]{0:T(128)S(1)} %stack.60.flag_ref, bf16[384,3072]{1,0:T(8,128)(2,1)S(1)} %collective-permute-done.40.value_ref, f32[768,3072]{1,0:T(8,128)} %place_half.4.refs_0_), custom_call_target="tpu_custom_call", output_to_operand_aliasing={{}: (2, {})} | custom-call | flops 1 | bytes 1 | tf_op jit(solution)/shard_map/place_half/pallas_call | solution.py:924
  284.3 2.9 place_half.7
  (133 shorter events, 49.0 us)
Async XLA Ops:
  25.5 7.9 %collective-permute-start = (bf16[16,896]{1,0:T(8,128)(2,1)S(1)}, bf16[16,896]{1,0:T(8,128)(2,1)S(1)}, u32[]{:S(2)}, u32[]{:S(2)}) collective-permute-start(bf16[16,896]{1,0:T(8,128)(2,1)S(1)} %summarize.1), channel_id=1, source_target_pairs={{0,16},{16,0},{1,17},{17,1},{2,18},{18,2},{3,19},{19,3},{4,20},{20... | collective-permute-start | bytes 86024 | tf_op jit(solution)/shard_map/ppermute | solution.py:971
  33.4 7.6 %collective-permute-start.1 = (bf16[1,2,16,896]{3,2,1,0:T(8,128)(2,1)S(1)}, bf16[1,2,16,896]{3,2,1,0:T(8,128)(2,1)S(1)}, u32[]{:S(2)}, u32[]{:S(2)}) collective-permute-start(bf16[1,2,16,896]{3,2,1,0:T(8,128)(2,1)S(1)} %pad_maximum_fusion.1), channel_id=1, source_target_pairs={{0,8},{1,9},{2,10},{3,11},{4,12},{5,13},{6,14},{7,15},{8,0},{9,1},... | collective-permute-start | bytes 172040 | tf_op jit(solution)/shard_map/ppermute | solution.py:971
  47.6 9.4 %collective-permute-start.3 = (bf16[4,2,16,896]{3,2,1,0:T(8,128)(2,1)S(1)}, bf16[4,2,16,896]{3,2,1,0:T(8,128)(2,1)S(1)}, u32[]{:S(2)}, u32[]{:S(2)}) collective-permute-start(bf16[4,2,16,896]{3,2,1,0:T(8,128)(2,1)S(1)} %constant_dynamic-update-slice_fusion.2), channel_id=1, source_target_pairs={{0,2},{1,3},{2,0},{3,1},{4,6},{5,7},{6,4},{7,5},{8,10},{9,11},{10,... | collective-permute-start | bytes 688136 | tf_op jit(solution)/shard_map/ppermute | solution.py:971
  57.0 8.4 %collective-permute-start.4 = (bf16[8,2,16,896]{3,2,1,0:T(8,128)(2,1)S(1)}, bf16[8,2,16,896]{3,2,1,0:T(8,128)(2,1)S(1)}, u32[]{:S(2)}, u32[]{:S(2)}) collective-permute-start(bf16[8,2,16,896]{3,2,1,0:T(8,128)(2,1)S(1)} %constant_dynamic-update-slice_fusion.4), channel_id=1, source_target_pairs={{0,1},{1,0},{2,3},{3,2},{4,5},{5,4},{6,7},{7,6},{8,9},{9,8},{10,11... | collective-permute-start | bytes 1376264 | tf_op jit(solution)/shard_map/ppermute | solution.py:971
  81.9 23.4 %collective-permute-start.13 = (bf16[192,3072]{1,0:T(8,128)(2,1)S(1)}, bf16[192,3072]{1,0:T(8,128)(2,1)S(1)}, u32[]{:S(2)}, u32[]{:S(2)}) collective-permute-start(bf16[192,3072]{1,0:T(8,128)(2,1)S(1)} %get-tuple-element.294), channel_id=1, source_target_pairs={{0,4},{1,3},{2,6},{3,1},{4,0},{5,7},{6,2},{7,5},{8,12},{9,11},{10,... | collective-permute-start | bytes 3538952 | tf_op jit(solution)/shard_map/ppermute | solution.py:977
  106.2 23.0 %collective-permute-start.15 = (bf16[96,3072]{1,0:T(8,128)(2,1)S(1)}, bf16[96,3072]{1,0:T(8,128)(2,1)S(1)}, u32[]{:S(2)}, u32[]{:S(2)}) collective-permute-start(bf16[96,3072]{1,0:T(8,128)(2,1)S(1)} %get-tuple-element.314), channel_id=1, source_target_pairs={{0,8},{1,5},{2,10},{3,7},{4,12},{5,1},{6,14},{7,3},{8,0},{9,13},{1... | collective-permute-start | bytes 1769480 | tf_op jit(solution)/shard_map/ppermute | solution.py:977
  110.1 26.1 %collective-permute-start.14 = (bf16[192,3072]{1,0:T(8,128)(2,1)S(1)}, bf16[192,3072]{1,0:T(8,128)(2,1)S(1)}, u32[]{:S(2)}, u32[]{:S(2)}) collective-permute-start(bf16[192,3072]{1,0:T(8,128)(2,1)S(1)} %get-tuple-element.323), channel_id=1, source_target_pairs={{0,4},{1,3},{2,6},{3,1},{4,0},{5,7},{6,2},{7,5},{8,12},{9,11},{10,... | collective-permute-start | bytes 3538952 | tf_op jit(solution)/shard_map/ppermute | solution.py:977
  130.0 7.6 %collective-permute-start.17 = (bf16[48,3072]{1,0:T(8,128)(2,1)S(1)}, bf16[48,3072]{1,0:T(8,128)(2,1)S(1)}, u32[]{:S(2)}, u32[]{:S(2)}) collective-permute-start(bf16[48,3072]{1,0:T(8,128)(2,1)S(1)} %get-tuple-element.337), channel_id=1, source_target_pairs={{0,2},{1,9},{2,0},{3,11},{4,6},{5,13},{6,4},{7,15},{8,10},{9,1},{1... | collective-permute-start | bytes 884744 | tf_op jit(solution)/shard_map/ppermute | solution.py:977
  135.6 8.8 %collective-permute-start.18 = (bf16[384,768]{1,0:T(8,128)(2,1)S(1)}, bf16[384,768]{1,0:T(8,128)(2,1)S(1)}, u32[]{:S(2)}, u32[]{:S(2)}) collective-permute-start(bf16[384,768]{1,0:T(8,128)(2,1)S(1)} %get-tuple-element.341), channel_id=1, source_target_pairs={{0,1},{1,0},{2,3},{3,2},{4,5},{5,4},{6,7},{7,6},{8,9},{9,8},{10,11... | collective-permute-start | bytes 1769480 | tf_op jit(solution)/shard_map/ppermute | solution.py:971
  135.7 10.1 %collective-permute-start.19 = (bf16[384,768]{1,0:T(8,128)(2,1)S(1)}, bf16[384,768]{1,0:T(8,128)(2,1)S(1)}, u32[]{:S(2)}, u32[]{:S(2)}) collective-permute-start(bf16[384,768]{1,0:T(8,128)(2,1)S(1)} %get-tuple-element.363), channel_id=1, source_target_pairs={{0,1},{1,0},{2,3},{3,2},{4,5},{5,4},{6,7},{7,6},{8,9},{9,8},{10,11... | collective-permute-start | bytes 1769480 | tf_op jit(solution)/shard_map/ppermute | solution.py:971
  136.2 9.6 %collective-permute-start.20 = (bf16[384,768]{1,0:T(8,128)(2,1)S(1)}, bf16[384,768]{1,0:T(8,128)(2,1)S(1)}, u32[]{:S(2)}, u32[]{:S(2)}) collective-permute-start(bf16[384,768]{1,0:T(8,128)(2,1)S(1)} %get-tuple-element.364), channel_id=1, source_target_pairs={{0,1},{1,0},{2,3},{3,2},{4,5},{5,4},{6,7},{7,6},{8,9},{9,8},{10,11... | collective-permute-start | bytes 1769480 | tf_op jit(solution)/shard_map/ppermute | solution.py:971
  136.2 9.5 %collective-permute-start.21 = (bf16[384,768]{1,0:T(8,128)(2,1)S(1)}, bf16[384,768]{1,0:T(8,128)(2,1)S(1)}, u32[]{:S(2)}, u32[]{:S(2)}) collective-permute-start(bf16[384,768]{1,0:T(8,128)(2,1)S(1)} %get-tuple-element.365), channel_id=1, source_target_pairs={{0,1},{1,0},{2,3},{3,2},{4,5},{5,4},{6,7},{7,6},{8,9},{9,8},{10,11... | collective-permute-start | bytes 1769480 | tf_op jit(solution)/shard_map/ppermute | solution.py:971
  137.6 23.2 %collective-permute-start.16 = (bf16[96,3072]{1,0:T(8,128)(2,1)S(1)}, bf16[96,3072]{1,0:T(8,128)(2,1)S(1)}, u32[]{:S(2)}, u32[]{:S(2)}) collective-permute-start(bf16[96,3072]{1,0:T(8,128)(2,1)S(1)} %get-tuple-element.345), channel_id=1, source_target_pairs={{0,8},{1,5},{2,10},{3,7},{4,12},{5,1},{6,14},{7,3},{8,0},{9,13},{1... | collective-permute-start | bytes 1769480 | tf_op jit(solution)/shard_map/ppermute | solution.py:977
  144.4 27.2 %collective-permute-start.24 = (bf16[48,3072]{1,0:T(8,128)(2,1)S(1)}, bf16[48,3072]{1,0:T(8,128)(2,1)S(1)}, u32[]{:S(2)}, u32[]{:S(2)}) collective-permute-start(bf16[48,3072]{1,0:T(8,128)(2,1)S(1)} %add.83.mine_ref), channel_id=1, source_target_pairs={{0,2},{1,9},{2,0},{3,11},{4,6},{5,13},{6,4},{7,15},{8,10},{9,1},{1... | collective-permute-start | bytes 884744 | tf_op jit(solution)/shard_map/ppermute | solution.py:977
  145.7 25.9 %collective-permute-start.25 = (f32[16,768]{1,0:T(8,128)S(1)}, f32[16,768]{1,0:T(8,128)S(1)}, u32[]{:S(2)}, u32[]{:S(2)}) collective-permute-start(f32[16,768]{1,0:T(8,128)S(1)} %pack_vectors.1.mine_ref), channel_id=1, source_target_pairs={{0,1},{1,0},{2,3},{3,2},{4,5},{5,4},{6,7},{7,6},{8,9},{9,8},{10,11... | collective-permute-start | bytes 147464 | tf_op jit(solution)/shard_map/ppermute | solution.py:971
  147.0 31.9 %collective-permute-start.22 = (bf16[192,3072]{1,0:T(8,128)(2,1)S(1)}, bf16[192,3072]{1,0:T(8,128)(2,1)S(1)}, u32[]{:S(2)}, u32[]{:S(2)}) collective-permute-start(bf16[192,3072]{1,0:T(8,128)(2,1)S(1)} %get-tuple-element.374), channel_id=1, source_target_pairs={{0,4},{1,3},{2,6},{3,1},{4,0},{5,7},{6,2},{7,5},{8,12},{9,11},{10,... | collective-permute-start | bytes 3538952 | tf_op jit(solution)/shard_map/ppermute | solution.py:977
  161.5 10.7 %collective-permute-start.23 = (bf16[48,3072]{1,0:T(8,128)(2,1)S(1)}, bf16[48,3072]{1,0:T(8,128)(2,1)S(1)}, u32[]{:S(2)}, u32[]{:S(2)}) collective-permute-start(bf16[48,3072]{1,0:T(8,128)(2,1)S(1)} %get-tuple-element.377), channel_id=1, source_target_pairs={{0,2},{1,9},{2,0},{3,11},{4,6},{5,13},{6,4},{7,15},{8,10},{9,1},{1... | collective-permute-start | bytes 884744 | tf_op jit(solution)/shard_map/ppermute | solution.py:977
  172.2 17.2 %collective-permute-start.27 = (bf16[96,3072]{1,0:T(8,128)(2,1)S(1)}, bf16[96,3072]{1,0:T(8,128)(2,1)S(1)}, u32[]{:S(2)}, u32[]{:S(2)}) collective-permute-start(bf16[96,3072]{1,0:T(8,128)(2,1)S(1)} %join.9.mine_ref), channel_id=1, source_target_pairs={{0,8},{1,5},{2,10},{3,7},{4,12},{5,1},{6,14},{7,3},{8,0},{9,13},{1... | collective-permute-start | bytes 1769480 | tf_op jit(solution)/shard_map/ppermute | solution.py:977
  179.8 33.6 %collective-permute-start.26 = (bf16[96,3072]{1,0:T(8,128)(2,1)S(1)}, bf16[96,3072]{1,0:T(8,128)(2,1)S(1)}, u32[]{:S(2)}, u32[]{:S(2)}) collective-permute-start(bf16[96,3072]{1,0:T(8,128)(2,1)S(1)} %get-tuple-element.391), channel_id=1, source_target_pairs={{0,8},{1,5},{2,10},{3,7},{4,12},{5,1},{6,14},{7,3},{8,0},{9,13},{1... | collective-permute-start | bytes 1769480 | tf_op jit(solution)/shard_map/ppermute | solution.py:977
  190.0 31.7 %collective-permute-start.31 = (bf16[192,3072]{1,0:T(8,128)(2,1)S(1)}, bf16[192,3072]{1,0:T(8,128)(2,1)S(1)}, u32[]{:S(2)}, u32[]{:S(2)}) collective-permute-start(bf16[192,3072]{1,0:T(8,128)(2,1)S(1)} %join.10.mine_ref), channel_id=1, source_target_pairs={{0,4},{1,3},{2,6},{3,1},{4,0},{5,7},{6,2},{7,5},{8,12},{9,11},{10,... | collective-permute-start | bytes 3538952 | tf_op jit(solution)/shard_map/ppermute | solution.py:977
  190.1 24.8 %collective-permute-start.29 = (bf16[48,3072]{1,0:T(8,128)(2,1)S(1)}, bf16[48,3072]{1,0:T(8,128)(2,1)S(1)}, u32[]{:S(2)}, u32[]{:S(2)}) collective-permute-start(bf16[48,3072]{1,0:T(8,128)(2,1)S(1)} %add.85.mine_ref), channel_id=1, source_target_pairs={{0,2},{1,9},{2,0},{3,11},{4,6},{5,13},{6,4},{7,15},{8,10},{9,1},{1... | collective-permute-start | bytes 884744 | tf_op jit(solution)/shard_map/ppermute | solution.py:977
  214.1 6.8 %collective-permute-start.28 = (bf16[48,3072]{1,0:T(8,128)(2,1)S(1)}, bf16[48,3072]{1,0:T(8,128)(2,1)S(1)}, u32[]{:S(2)}, u32[]{:S(2)}) collective-permute-start(bf16[48,3072]{1,0:T(8,128)(2,1)S(1)} %get-tuple-element.397), channel_id=1, source_target_pairs={{0,2},{1,9},{2,0},{3,11},{4,6},{5,13},{6,4},{7,15},{8,10},{9,1},{1... | collective-permute-start | bytes 884744 | tf_op jit(solution)/shard_map/ppermute | solution.py:977
  221.0 6.8 %collective-permute-start.30 = (bf16[48,3072]{1,0:T(8,128)(2,1)S(1)}, bf16[48,3072]{1,0:T(8,128)(2,1)S(1)}, u32[]{:S(2)}, u32[]{:S(2)}) collective-permute-start(bf16[48,3072]{1,0:T(8,128)(2,1)S(1)} %add.86.mine_ref), channel_id=1, source_target_pairs={{0,2},{1,9},{2,0},{3,11},{4,6},{5,13},{6,4},{7,15},{8,10},{9,1},{1... | collective-permute-start | bytes 884744 | tf_op jit(solution)/shard_map/ppermute | solution.py:977
  221.7 20.7 %collective-permute-start.34 = (bf16[96,3072]{1,0:T(8,128)(2,1)S(1)}, bf16[96,3072]{1,0:T(8,128)(2,1)S(1)}, u32[]{:S(2)}, u32[]{:S(2)}) collective-permute-start(bf16[96,3072]{1,0:T(8,128)(2,1)S(1)} %join.11.mine_ref), channel_id=1, source_target_pairs={{0,8},{1,5},{2,10},{3,7},{4,12},{5,1},{6,14},{7,3},{8,0},{9,13},{1... | collective-permute-start | bytes 1769480 | tf_op jit(solution)/shard_map/ppermute | solution.py:977
  222.4 31.7 %collective-permute-start.38 = (bf16[384,3072]{1,0:T(8,128)(2,1)S(1)}, bf16[384,3072]{1,0:T(8,128)(2,1)S(1)}, u32[]{:S(2)}, u32[]{:S(2)}) collective-permute-start(bf16[384,3072]{1,0:T(8,128)(2,1)S(1)} %join.12.value_ref), channel_id=1, source_target_pairs={{0,1},{1,0},{2,3},{3,2},{4,5},{5,4},{6,7},{7,6},{8,9},{9,8},{10,11... | collective-permute-start | bytes 7077896 | tf_op jit(solution)/shard_map/ppermute | solution.py:971
  228.4 23.0 %collective-permute-start.32 = (bf16[96,3072]{1,0:T(8,128)(2,1)S(1)}, bf16[96,3072]{1,0:T(8,128)(2,1)S(1)}, u32[]{:S(2)}, u32[]{:S(2)}) collective-permute-start(bf16[96,3072]{1,0:T(8,128)(2,1)S(1)} %join.13.mine_ref), channel_id=1, source_target_pairs={{0,8},{1,5},{2,10},{3,7},{4,12},{5,1},{6,14},{7,3},{8,0},{9,13},{1... | collective-permute-start | bytes 1769480 | tf_op jit(solution)/shard_map/ppermute | solution.py:977
  229.4 13.7 %collective-permute-start.33 = (f32[16,768]{1,0:T(8,128)S(1)}, f32[16,768]{1,0:T(8,128)S(1)}, u32[]{:S(2)}, u32[]{:S(2)}) collective-permute-start(f32[16,768]{1,0:T(8,128)S(1)} %add.84.mine_ref), channel_id=1, source_target_pairs={{0,2},{1,3},{2,0},{3,1},{4,6},{5,7},{6,4},{7,5},{8,10},{9,11},{10,... | collective-permute-start | bytes 147464 | tf_op jit(solution)/shard_map/ppermute | solution.py:971
  243.0 21.5 %collective-permute-start.37 = (bf16[192,3072]{1,0:T(8,128)(2,1)S(1)}, bf16[192,3072]{1,0:T(8,128)(2,1)S(1)}, u32[]{:S(2)}, u32[]{:S(2)}) collective-permute-start(bf16[192,3072]{1,0:T(8,128)(2,1)S(1)} %join.14.mine_ref), channel_id=1, source_target_pairs={{0,4},{1,3},{2,6},{3,1},{4,0},{5,7},{6,2},{7,5},{8,12},{9,11},{10,... | collective-permute-start | bytes 3538952 | tf_op jit(solution)/shard_map/ppermute | solution.py:977
  252.1 25.6 %collective-permute-start.35 = (bf16[192,3072]{1,0:T(8,128)(2,1)S(1)}, bf16[192,3072]{1,0:T(8,128)(2,1)S(1)}, u32[]{:S(2)}, u32[]{:S(2)}) collective-permute-start(bf16[192,3072]{1,0:T(8,128)(2,1)S(1)} %join.15.mine_ref), channel_id=1, source_target_pairs={{0,4},{1,3},{2,6},{3,1},{4,0},{5,7},{6,2},{7,5},{8,12},{9,11},{10,... | collective-permute-start | bytes 3538952 | tf_op jit(solution)/shard_map/ppermute | solution.py:977
  252.1 25.5 %collective-permute-start.36 = (f32[16,768]{1,0:T(8,128)S(1)}, f32[16,768]{1,0:T(8,128)S(1)}, u32[]{:S(2)}, u32[]{:S(2)}) collective-permute-start(f32[16,768]{1,0:T(8,128)S(1)} %add.87.mine_ref), channel_id=1, source_target_pairs={{0,4},{1,5},{2,6},{3,7},{4,0},{5,1},{6,2},{7,3},{8,12},{9,13},{10,... | collective-permute-start | bytes 147464 | tf_op jit(solution)/shard_map/ppermute | solution.py:971
  265.2 16.2 %collective-permute-start.40 = (bf16[384,3072]{1,0:T(8,128)(2,1)S(1)}, bf16[384,3072]{1,0:T(8,128)(2,1)S(1)}, u32[]{:S(2)}, u32[]{:S(2)}) collective-permute-start(bf16[384,3072]{1,0:T(8,128)(2,1)S(1)} %join.16.value_ref), channel_id=1, source_target_pairs={{0,1},{1,0},{2,3},{3,2},{4,5},{5,4},{6,7},{7,6},{8,9},{9,8},{10,11... | collective-permute-start | bytes 7077896 | tf_op jit(solution)/shard_map/ppermute | solution.py:971
  278.5 8.7 %collective-permute-start.41 = (f32[16,768]{1,0:T(8,128)S(1)}, f32[16,768]{1,0:T(8,128)S(1)}, u32[]{:S(2)}, u32[]{:S(2)}) collective-permute-start(f32[16,768]{1,0:T(8,128)S(1)} %add.88.mine_ref), channel_id=1, source_target_pairs={{0,8},{1,9},{2,10},{3,11},{4,12},{5,13},{6,14},{7,15},{8,0},{9,1},... | collective-permute-start | bytes 147464 | tf_op jit(solution)/shard_map/ppermute | solution.py:971
  (20 other events, 131.8 us)

commit v2 on v1

--- a/solution.py
+++ b/solution.py
@@ -267,7 +267,7 @@
         out_ref[:, width:] = digits.astype(FLOAT_KIND).astype(BRAIN)
 
 
-def summarize(enc, starts, targets, normal, first, expand, lift, shrink, settle, second, tn=1024):
+def summarize(enc, starts, targets, normal, first, expand, lift, shrink, settle, second, tn=1536):
     count, width = normal.shape
     hidden = expand.shape[1]
     slots = starts.shape[0]
@@ -299,7 +299,7 @@
         ),
         out_shape=jax.ShapeDtypeStruct((slots, width + LANES), BRAIN),
         cost_estimate=cost(1, 1),
-        compiler_params=pltpu.CompilerParams(vmem_limit_bytes=10 * MEGA),
+        compiler_params=pltpu.CompilerParams(vmem_limit_bytes=15 * MEGA),
         name="summarize",
     )(
         enc,

time: 288 us -> 288 us (level)
  no operation moved by 1% of the time
where the time goes in v2:
time: 288 us; the launch traced here: 287 us
  Pallas kernels  153 us (53%)
  waiting for transfers between devices  97.3 us (34%)
  starting transfers between devices  29 us (10%)
  local copies, waits for them, and re-layouts  5.44 us (2%)
    ppermute x18, waiting for transfers between devices, swapped_by_core(): return lax.ppermute(value, 'batch', pairs)  85.8 us
    pallas_call x1, Pallas kernels, feed_back(): pl.pallas_call(feed_kernel, grid_spec=pltpu.PrefetchScalarGridSpec(num_sc...  21.2 us
    pallas_call x4, Pallas kernels, widen(): pl.pallas_call(widen_kernel, grid=(steps,), in_specs=[whole(low.shape), c...  19.7 us
    pallas_call x1, Pallas kernels, attend(): pl.pallas_call(attend_kernel, grid_spec=pltpu.PrefetchScalarGridSpec(num_...  17.7 us
    pallas_call x1, Pallas kernels, attend_back(): pl.pallas_call(attend_back_kernel, grid=(count // ROWS,), in_specs=[row_b...  16.2 us
    ppermute x24, starting transfers between devices, swapped(): return lax.ppermute(value, axis, pairs)  15.9 us
    ppermute x18, starting transfers between devices, swapped_by_core(): return lax.ppermute(value, 'batch', pairs)  13.1 us
    pallas_call x4, Pallas kernels, place_half(): pl.pallas_call(functools.partial(place_kernel, kept=len(kept)), grid_spec...  11.5 us
  transfers between devices with their start and end apart: 42, of which 13 were waited for; matrix products, arithmetic and copies ran while one was open for 0% of the time, Pallas kernels for 41%

profile of v2, /device:TPU:0, one launch (start us, length us, event | category | flops | bytes accessed | tf_op | source)
XLA Modules:
  0.0 287.0 jit_solution(7253731450530182157)
XLA Ops:
  1.9 17.7 %attend.1 = (bf16[1024,2304]{1,0:T(8,128)(2,1)S(1)}, bf16[4,6,256,512]{3,2,1,0:T(8,128)(2,1)S(1)}, bf16[1024,768]{1,0:T(8,128)(2,1)S(1)}, f32[1024,768]{1,0:T(8,...) custom-call(s32[12]{0:T(128)S(1)} %stack.60.flag_ref, bf16[1024,768]{1,0:T(8,128)(2,1)} %bitcast.51, ...), custom_call_target="tpu_custom_call" | custom-call | flops 1 | bytes 1 | tf_op jit(solution)/shard_map/attend/pallas_call | solution.py:173
  19.6 5.1 %summarize.1 = bf16[16,896]{1,0:T(8,128)(2,1)S(1)} custom-call(s32[12]{0:T(128)S(1)} %stack.60.flag_ref, s32[16]{0:T(128)S(1)} %copy-done.4, s32[16]{0:T(128)S(1)} %copy-done.5, f32[128,8,768]{2,1,0:T(8,128)S(1)} %bitcast.41, bf16[1,768]{1,0:T(2,128)(2,1)} %gain_ref.5, bf16[1,768]{1,0:T(2,128)(2,1)} %shift_one_ref.3, bf16[768,3072]{1,0:T(8,128)(2,1)S(1)} %bitcast.30, ...), custom_call_target="tpu_custom_call" | custom-call | flops 1 | bytes 1 | tf_op jit(solution)/shard_map/summarize/pallas_call | solution.py:275
  24.7 3.0 %collective-permute-start = (bf16[16,896]{1,0:T(8,128)(2,1)S(1)}, bf16[16,896]{1,0:T(8,128)(2,1)S(1)}, u32[]{:S(2)}, u32[]{:S(2)}) collective-permute-start(bf16[16,896]{1,0:T(8,128)(2,1)S(1)} %summarize.1), channel_id=1, source_target_pairs={{0,16},{16,0},{1,17},{17,1},{2,18},{18,2},{3,19},{19,3},{4,20},{20... | collective-permute-start | bytes 86024 | tf_op jit(solution)/shard_map/ppermute | solution.py:971
  27.7 4.9 %widen.4 = (bf16[1024,3072]{1,0:T(8,128)(2,1)S(1)}, bf16[1024,3072]{1,0:T(8,128)(2,1)S(1)}) custom-call(bf16[1024,768]{1,0:T(8,128)(2,1)S(1)} %get-tuple-element.251.low_ref, bf16[768,3072]{1,0:T(8,128)(2,1)S(1)} %bitcast.31, bf16[1,3072]{1,0:T(2,128)(2,1)} %lift_ref.9), custom_call_target="tpu_custom_call" | custom-call | flops 1 | bytes 1 | tf_op jit(solution)/shard_map/widen/pallas_call | solution.py:336
  35.3 4.9 %widen.5 = (bf16[1024,3072]{1,0:T(8,128)(2,1)S(1)}, bf16[1024,3072]{1,0:T(8,128)(2,1)S(1)}) custom-call(bf16[1024,768]{1,0:T(8,128)(2,1)S(1)} %get-tuple-element.251.low_ref, bf16[768,3072]{1,0:T(8,128)(2,1)S(1)} %bitcast.32, bf16[1,3072]{1,0:T(2,128)(2,1)} %lift_ref.9, ...), custom_call_target="tpu_custom_call", output_to_operand_aliasing={{0}: (3, {}), {1}: (4, {})} | custom-call | flops 1 | bytes 1 | tf_op jit(solution)/shard_map/widen/pallas_call | solution.py:336
  41.9 4.9 %widen.6 = (bf16[1024,3072]{1,0:T(8,128)(2,1)S(1)}, bf16[1024,3072]{1,0:T(8,128)(2,1)S(1)}) custom-call(bf16[1024,768]{1,0:T(8,128)(2,1)S(1)} %get-tuple-element.251.low_ref, bf16[768,3072]{1,0:T(8,128)(2,1)S(1)} %bitcast.33, bf16[1,3072]{1,0:T(2,128)(2,1)} %lift_ref.9, ...), custom_call_target="tpu_custom_call", output_to_operand_aliasing={{0}: (3, {}), {1}: (4, {})} | custom-call | flops 1 | bytes 1 | tf_op jit(solution)/shard_map/widen/pallas_call | solution.py:336
  48.4 5.0 %widen.7 = (bf16[1024,3072]{1,0:T(8,128)(2,1)S(1)}, bf16[1024,3072]{1,0:T(8,128)(2,1)S(1)}) custom-call(bf16[1024,768]{1,0:T(8,128)(2,1)S(1)} %get-tuple-element.251.low_ref, bf16[768,3072]{1,0:T(8,128)(2,1)S(1)} %bitcast.34, bf16[1,3072]{1,0:T(2,128)(2,1)} %lift_ref.9, ...), custom_call_target="tpu_custom_call", output_to_operand_aliasing={{0}: (3, {}), {1}: (4, {})} | custom-call | flops 1 | bytes 1 | tf_op jit(solution)/shard_map/widen/pallas_call | solution.py:336
  53.5 2.7 copy-done.2
  56.4 8.3 %shrink.1 = (f32[1024,768]{1,0:T(8,128)S(1)}, f32[1024,1]{1,0:T(8,128)S(1)}, bf16[1024,768]{1,0:T(8,128)(2,1)}) custom-call(bf16[1024,3072]{1,0:T(8,128)(2,1)S(1)} %get-tuple-element.278.active_ref, bf16[3072,768]{1,0:T(8,128)(2,1)S(1)} %bitcast.40, f32[1024,768]{1,0:T(8,128)S(1)} %get-tuple-element.325.normal_ref, bf16[1,768]{1,0:T(2,128)(2,1)} %gain_ref.5, ...), custom_call_target="tpu_custom_call" | custom-call | flops 1 | bytes 1 | tf_op jit(solution)/shard_map/shrink/pallas_call | solution.py:375
  64.7 5.5 %contrast.1 = (f32[1024,768]{1,0:T(8,128)S(1)}, bf16[1024,768]{1,0:T(8,128)(2,1)S(1)}, f32[8,768]{1,0:T(8,128)S(1)}) custom-call(s32[12]{0:T(128)S(1)} %stack.60.flag_ref, s32[16]{0:T(128)S(1)} %copy-done.4, bf16[16,2,16,896]{3,2,1,0:T(8,128)(2,1)S(1)} %pad_maximum_fusion.every_ref, s32[1,256]{1,0:T(1,128)S(1)} %select_n.48.column_ref, ...), custom_call_target="tpu_custom_call" | custom-call | flops 1 | bytes 1 | tf_op jit(solution)/shard_map/contrast/pallas_call | solution.py:490
  70.2 4.2 %contraction_half.2 = (bf16[384,768]{1,0:T(8,128)(2,1)S(1)}, bf16[384,768]{1,0:T(8,128)(2,1)S(1)}, bf16[384,768]{1,0:T(8,128)(2,1)S(1)}, bf16[384,768]{1,0:T(8,128)(2,1)S(1)}) custom-call(s32[1]{0:T(128)S(6)} %sub.7.flag_ref, bf16[1024,768]{1,0:T(8,128)(2,1)S(1)} %get-tuple-element.295.low_ref.two_low_ref, bf16[1024,3072]{1,0:T(8,128)(2,1)S(1)} %get-tuple-element.278.active_ref), custom_call_target="tpu_custom_call" | custom-call | flops 99999997952 | bytes 1 | tf_op jit(solution)/shard_map/contraction_half/pallas_call | solution.py:541
  75.6 4.2 %contraction_half.3 = (bf16[384,768]{1,0:T(8,128)(2,1)S(1)}, bf16[384,768]{1,0:T(8,128)(2,1)S(1)}, bf16[384,768]{1,0:T(8,128)(2,1)S(1)}, bf16[384,768]{1,0:T(8,128)(2,1)S(1)}) custom-call(s32[1]{0:T(128)} %bitcast.1.flag_ref, bf16[1024,768]{1,0:T(8,128)(2,1)S(1)} %get-tuple-element.295.low_ref.two_low_ref, bf16[1024,3072]{1,0:T(8,128)(2,1)S(1)} %get-tuple-element.278.active_ref), custom_call_target="tpu_custom_call" | custom-call | flops 99999997952 | bytes 1 | tf_op jit(solution)/shard_map/contraction_half/pallas_call | solution.py:541
  82.2 21.2 %feed_back.1 = (f32[1,3072]{1,0:T(1,128)S(1)}, f32[1024,768]{1,0:T(8,128)S(1)}, bf16[384,768]{1,0:T(8,128)(2,1)S(1)}, bf16[384,768]{1,0:T(8,128)(2,1)S(1)}, bf16...) custom-call(s32[12]{0:T(128)S(1)} %stack.60.flag_ref, ...), custom_call_target="tpu_custom_call" | custom-call | flops 6000000000 | bytes 1 | tf_op jit(solution)/shard_map/feed_back/pallas_call | solution.py:605
  112.3 16.2 %attend_back.1 = (f32[1024,768]{1,0:T(8,128)S(1)}, bf16[1024,768]{1,0:T(8,128)(2,1)S(1)}, bf16[1024,2304]{1,0:T(8,128)(2,1)S(1)}, f32[8,768]{1,0:T(8,128)S(1)}, f32[1,2304]{1,0:T(1,128)S(1)}) custom-call(f32[1024,768]{1,0:T(8,128)S(1)} %copy-done.7, f32[1024,768]{1,0:T(8,128)S(1)} %get-tuple-element.325.normal_ref, ...), custom_call_target="tpu_custom_call" | custom-call | flops 6000000000 | bytes 1 | tf_op jit(solution)/shard_map/attend_back/pallas_call | solution.py:691
  129.8 5.0 %merge_project_half.2 = (bf16[384,768]{1,0:T(8,128)(2,1)S(1)}, bf16[384,768]{1,0:T(8,128)(2,1)S(1)}, bf16[384,768]{1,0:T(8,128)(2,1)S(1)}, bf16[384,768]{1,0:T(8,128)(2,1)S(1)}) custom-call(s32[1]{0:T(128)S(6)} %sub.7.flag_ref, bf16[1024,768]{1,0:T(8,128)(2,1)S(1)} %get-tuple-element.356.context_ref, bf16[1024,768]{1,0:T(8,128)(2,1)S(1)} %get-tuple-element.357.one_ref, ...), custom_call_target="tpu_custom_call" | custom-call | flops 20000000000 | bytes 1 | tf_op jit(solution)/shard_map/merge_project_half/pallas_call | solution.py:747
  138.5 5.0 %merge_project_half.3 = (bf16[384,768]{1,0:T(8,128)(2,1)S(1)}, bf16[384,768]{1,0:T(8,128)(2,1)S(1)}, bf16[384,768]{1,0:T(8,128)(2,1)S(1)}, bf16[384,768]{1,0:T(8,128)(2,1)S(1)}) custom-call(s32[1]{0:T(128)} %bitcast.1.flag_ref, bf16[1024,768]{1,0:T(8,128)(2,1)S(1)} %get-tuple-element.356.context_ref, bf16[1024,768]{1,0:T(8,128)(2,1)S(1)} %get-tuple-element.357.one_ref, ...), custom_call_target="tpu_custom_call" | custom-call | flops 20000000000 | bytes 1 | tf_op jit(solution)/shard_map/merge_project_half/pallas_call | solution.py:747
  147.1 12.9 %collective-permute-done.16.refs_1_ = bf16[96,3072]{1,0:T(8,128)(2,1)S(1)} collective-permute-done((bf16[96,3072]{1,0:T(8,128)(2,1)S(1)}, bf16[96,3072]{1,0:T(8,128)(2,1)S(1)}, u32[]{:S(2)}, u32[]{:S(2)}) %collective-permute-start.16) | collective-permute-done | bytes 589856 | tf_op jit(solution)/shard_map/ppermute | solution.py:977
  163.4 7.4 %tokens_back.1 = f32[1024,768]{1,0:T(8,128)} custom-call(f32[1024,768]{1,0:T(8,128)S(1)} %get-tuple-element.378.one_ref, bf16[1024,2304]{1,0:T(8,128)(2,1)S(1)} %get-tuple-element.379.packed_ref, bf16[768,2304]{1,0:T(8,128)(2,1)} %bitcast.46), custom_call_target="tpu_custom_call" | custom-call | flops 1 | bytes 1 | tf_op jit(solution)/shard_map/tokens_back/pallas_call | solution.py:851
  171.6 6.5 %collective-permute-done.22.refs_1_ = bf16[192,3072]{1,0:T(8,128)(2,1)S(1)} collective-permute-done((bf16[192,3072]{1,0:T(8,128)(2,1)S(1)}, bf16[192,3072]{1,0:T(8,128)(2,1)S(1)}, u32[]{:S(2)}, u32[]{:S(2)}) %collective-permute-start.22) | collective-permute-done | bytes 1179680 | tf_op jit(solution)/shard_map/ppermute | solution.py:977
  179.1 9.5 %collective-permute-done.27.other_ref = bf16[96,3072]{1,0:T(8,128)(2,1)S(1)} collective-permute-done((bf16[96,3072]{1,0:T(8,128)(2,1)S(1)}, bf16[96,3072]{1,0:T(8,128)(2,1)S(1)}, u32[]{:S(2)}, u32[]{:S(2)}) %collective-permute-start.27) | collective-permute-done | bytes 589856 | tf_op jit(solution)/shard_map/ppermute | solution.py:977
  190.3 22.4 %collective-permute-done.26.refs_1_ = bf16[96,3072]{1,0:T(8,128)(2,1)S(1)} collective-permute-done((bf16[96,3072]{1,0:T(8,128)(2,1)S(1)}, bf16[96,3072]{1,0:T(8,128)(2,1)S(1)}, u32[]{:S(2)}, u32[]{:S(2)}) %collective-permute-start.26) | collective-permute-done | bytes 589856 | tf_op jit(solution)/shard_map/ppermute | solution.py:977
  214.6 5.5 %collective-permute-done.28.other_ref = bf16[48,3072]{1,0:T(8,128)(2,1)S(1)} collective-permute-done((bf16[48,3072]{1,0:T(8,128)(2,1)S(1)}, bf16[48,3072]{1,0:T(8,128)(2,1)S(1)}, u32[]{:S(2)}, u32[]{:S(2)}) %collective-permute-start.28) | collective-permute-done | bytes 294944 | tf_op jit(solution)/shard_map/ppermute | solution.py:977
  221.7 3.3 %place_turned_half.2.refs_0_ = f32[3072,768]{1,0:T(8,128)} custom-call(s32[12]{0:T(128)S(1)} %stack.60.flag_ref, bf16[384,3072]{1,0:T(8,128)(2,1)S(1)} %join.12.value_ref), custom_call_target="tpu_custom_call" | custom-call | flops 1 | bytes 1 | tf_op jit(solution)/shard_map/place_turned_half/pallas_call | solution.py:951
  230.0 11.6 %collective-permute-done.34.other_ref = bf16[96,3072]{1,0:T(8,128)(2,1)S(1)} collective-permute-done((bf16[96,3072]{1,0:T(8,128)(2,1)S(1)}, bf16[96,3072]{1,0:T(8,128)(2,1)S(1)}, u32[]{:S(2)}, u32[]{:S(2)}) %collective-permute-start.34) | collective-permute-done | bytes 589856 | tf_op jit(solution)/shard_map/ppermute | solution.py:977
  242.3 8.3 %collective-permute-done.32.other_ref = bf16[96,3072]{1,0:T(8,128)(2,1)S(1)} collective-permute-done((bf16[96,3072]{1,0:T(8,128)(2,1)S(1)}, bf16[96,3072]{1,0:T(8,128)(2,1)S(1)}, u32[]{:S(2)}, u32[]{:S(2)}) %collective-permute-start.32) | collective-permute-done | bytes 589856 | tf_op jit(solution)/shard_map/ppermute | solution.py:977
  253.4 3.3 %place_turned_half.3 = f32[3072,768]{1,0:T(8,128)} custom-call(s32[12]{0:T(128)S(1)} %stack.60.flag_ref, bf16[384,3072]{1,0:T(8,128)(2,1)S(1)} %collective-permute-done.38.value_ref, f32[3072,768]{1,0:T(8,128)} %place_turned_half.2.refs_0_), custom_call_target="tpu_custom_call", output_to_operand_aliasing={{}: (2, {})} | custom-call | flops 1 | bytes 1 | tf_op jit(solution)/shard_map/place_turned_half/pallas_call | solution.py:951
  256.7 7.1 %collective-permute-done.37.other_ref = bf16[192,3072]{1,0:T(8,128)(2,1)S(1)} collective-permute-done((bf16[192,3072]{1,0:T(8,128)(2,1)S(1)}, bf16[192,3072]{1,0:T(8,128)(2,1)S(1)}, u32[]{:S(2)}, u32[]{:S(2)}) %collective-permute-start.37) | collective-permute-done | bytes 1179680 | tf_op jit(solution)/shard_map/ppermute | solution.py:977
  264.5 2.9 %place_half.4.refs_0_ = f32[768,3072]{1,0:T(8,128)} custom-call(s32[12]{0:T(128)S(1)} %stack.60.flag_ref, bf16[384,3072]{1,0:T(8,128)(2,1)S(1)} %join.16.value_ref), custom_call_target="tpu_custom_call" | custom-call | flops 1 | bytes 1 | tf_op jit(solution)/shard_map/place_half/pallas_call | solution.py:924
  267.4 9.5 %collective-permute-done.36.other_ref = f32[16,768]{1,0:T(8,128)S(1)} collective-permute-done((f32[16,768]{1,0:T(8,128)S(1)}, f32[16,768]{1,0:T(8,128)S(1)}, u32[]{:S(2)}, u32[]{:S(2)}) %collective-permute-start.36) | collective-permute-done | bytes 49184 | tf_op jit(solution)/shard_map/ppermute | solution.py:971
  277.8 2.9 place_half.5
  280.6 2.9 %place_half.6 = f32[768,3072]{1,0:T(8,128)} custom-call(s32[12]{0:T(128)S(1)} %stack.60.flag_ref, bf16[384,3072]{1,0:T(8,128)(2,1)S(1)} %collective-permute-done.40.value_ref, f32[768,3072]{1,0:T(8,128)} %place_half.4.refs_0_), custom_call_target="tpu_custom_call", output_to_operand_aliasing={{}: (2, {})} | custom-call | flops 1 | bytes 1 | tf_op jit(solution)/shard_map/place_half/pallas_call | solution.py:924
  283.5 2.9 place_half.7
  (133 shorter events, 49.0 us)
Async XLA Ops:
  24.7 7.9 %collective-permute-start = (bf16[16,896]{1,0:T(8,128)(2,1)S(1)}, bf16[16,896]{1,0:T(8,128)(2,1)S(1)}, u32[]{:S(2)}, u32[]{:S(2)}) collective-permute-start(bf16[16,896]{1,0:T(8,128)(2,1)S(1)} %summarize.1), channel_id=1, source_target_pairs={{0,16},{16,0},{1,17},{17,1},{2,18},{18,2},{3,19},{19,3},{4,20},{20... | collective-permute-start | bytes 86024 | tf_op jit(solution)/shard_map/ppermute | solution.py:971
  32.6 7.6 %collective-permute-start.1 = (bf16[1,2,16,896]{3,2,1,0:T(8,128)(2,1)S(1)}, bf16[1,2,16,896]{3,2,1,0:T(8,128)(2,1)S(1)}, u32[]{:S(2)}, u32[]{:S(2)}) collective-permute-start(bf16[1,2,16,896]{3,2,1,0:T(8,128)(2,1)S(1)} %pad_maximum_fusion.1), channel_id=1, source_target_pairs={{0,8},{1,9},{2,10},{3,11},{4,12},{5,13},{6,14},{7,15},{8,0},{9,1},... | collective-permute-start | bytes 172040 | tf_op jit(solution)/shard_map/ppermute | solution.py:971
  46.8 9.4 %collective-permute-start.3 = (bf16[4,2,16,896]{3,2,1,0:T(8,128)(2,1)S(1)}, bf16[4,2,16,896]{3,2,1,0:T(8,128)(2,1)S(1)}, u32[]{:S(2)}, u32[]{:S(2)}) collective-permute-start(bf16[4,2,16,896]{3,2,1,0:T(8,128)(2,1)S(1)} %constant_dynamic-update-slice_fusion.2), channel_id=1, source_target_pairs={{0,2},{1,3},{2,0},{3,1},{4,6},{5,7},{6,4},{7,5},{8,10},{9,11},{10,... | collective-permute-start | bytes 688136 | tf_op jit(solution)/shard_map/ppermute | solution.py:971
  56.2 8.4 %collective-permute-start.4 = (bf16[8,2,16,896]{3,2,1,0:T(8,128)(2,1)S(1)}, bf16[8,2,16,896]{3,2,1,0:T(8,128)(2,1)S(1)}, u32[]{:S(2)}, u32[]{:S(2)}) collective-permute-start(bf16[8,2,16,896]{3,2,1,0:T(8,128)(2,1)S(1)} %constant_dynamic-update-slice_fusion.4), channel_id=1, source_target_pairs={{0,1},{1,0},{2,3},{3,2},{4,5},{5,4},{6,7},{7,6},{8,9},{9,8},{10,11... | collective-permute-start | bytes 1376264 | tf_op jit(solution)/shard_map/ppermute | solution.py:971
  81.1 23.4 %collective-permute-start.13 = (bf16[192,3072]{1,0:T(8,128)(2,1)S(1)}, bf16[192,3072]{1,0:T(8,128)(2,1)S(1)}, u32[]{:S(2)}, u32[]{:S(2)}) collective-permute-start(bf16[192,3072]{1,0:T(8,128)(2,1)S(1)} %get-tuple-element.294), channel_id=1, source_target_pairs={{0,4},{1,3},{2,6},{3,1},{4,0},{5,7},{6,2},{7,5},{8,12},{9,11},{10,... | collective-permute-start | bytes 3538952 | tf_op jit(solution)/shard_map/ppermute | solution.py:977
  105.4 23.0 %collective-permute-start.15 = (bf16[96,3072]{1,0:T(8,128)(2,1)S(1)}, bf16[96,3072]{1,0:T(8,128)(2,1)S(1)}, u32[]{:S(2)}, u32[]{:S(2)}) collective-permute-start(bf16[96,3072]{1,0:T(8,128)(2,1)S(1)} %get-tuple-element.314), channel_id=1, source_target_pairs={{0,8},{1,5},{2,10},{3,7},{4,12},{5,1},{6,14},{7,3},{8,0},{9,13},{1... | collective-permute-start | bytes 1769480 | tf_op jit(solution)/shard_map/ppermute | solution.py:977
  109.3 26.1 %collective-permute-start.14 = (bf16[192,3072]{1,0:T(8,128)(2,1)S(1)}, bf16[192,3072]{1,0:T(8,128)(2,1)S(1)}, u32[]{:S(2)}, u32[]{:S(2)}) collective-permute-start(bf16[192,3072]{1,0:T(8,128)(2,1)S(1)} %get-tuple-element.323), channel_id=1, source_target_pairs={{0,4},{1,3},{2,6},{3,1},{4,0},{5,7},{6,2},{7,5},{8,12},{9,11},{10,... | collective-permute-start | bytes 3538952 | tf_op jit(solution)/shard_map/ppermute | solution.py:977
  129.2 7.6 %collective-permute-start.17 = (bf16[48,3072]{1,0:T(8,128)(2,1)S(1)}, bf16[48,3072]{1,0:T(8,128)(2,1)S(1)}, u32[]{:S(2)}, u32[]{:S(2)}) collective-permute-start(bf16[48,3072]{1,0:T(8,128)(2,1)S(1)} %get-tuple-element.337), channel_id=1, source_target_pairs={{0,2},{1,9},{2,0},{3,11},{4,6},{5,13},{6,4},{7,15},{8,10},{9,1},{1... | collective-permute-start | bytes 884744 | tf_op jit(solution)/shard_map/ppermute | solution.py:977
  134.8 8.8 %collective-permute-start.18 = (bf16[384,768]{1,0:T(8,128)(2,1)S(1)}, bf16[384,768]{1,0:T(8,128)(2,1)S(1)}, u32[]{:S(2)}, u32[]{:S(2)}) collective-permute-start(bf16[384,768]{1,0:T(8,128)(2,1)S(1)} %get-tuple-element.341), channel_id=1, source_target_pairs={{0,1},{1,0},{2,3},{3,2},{4,5},{5,4},{6,7},{7,6},{8,9},{9,8},{10,11... | collective-permute-start | bytes 1769480 | tf_op jit(solution)/shard_map/ppermute | solution.py:971
  134.9 10.1 %collective-permute-start.19 = (bf16[384,768]{1,0:T(8,128)(2,1)S(1)}, bf16[384,768]{1,0:T(8,128)(2,1)S(1)}, u32[]{:S(2)}, u32[]{:S(2)}) collective-permute-start(bf16[384,768]{1,0:T(8,128)(2,1)S(1)} %get-tuple-element.363), channel_id=1, source_target_pairs={{0,1},{1,0},{2,3},{3,2},{4,5},{5,4},{6,7},{7,6},{8,9},{9,8},{10,11... | collective-permute-start | bytes 1769480 | tf_op jit(solution)/shard_map/ppermute | solution.py:971
  135.4 9.6 %collective-permute-start.20 = (bf16[384,768]{1,0:T(8,128)(2,1)S(1)}, bf16[384,768]{1,0:T(8,128)(2,1)S(1)}, u32[]{:S(2)}, u32[]{:S(2)}) collective-permute-start(bf16[384,768]{1,0:T(8,128)(2,1)S(1)} %get-tuple-element.364), channel_id=1, source_target_pairs={{0,1},{1,0},{2,3},{3,2},{4,5},{5,4},{6,7},{7,6},{8,9},{9,8},{10,11... | collective-permute-start | bytes 1769480 | tf_op jit(solution)/shard_map/ppermute | solution.py:971
  135.5 9.5 %collective-permute-start.21 = (bf16[384,768]{1,0:T(8,128)(2,1)S(1)}, bf16[384,768]{1,0:T(8,128)(2,1)S(1)}, u32[]{:S(2)}, u32[]{:S(2)}) collective-permute-start(bf16[384,768]{1,0:T(8,128)(2,1)S(1)} %get-tuple-element.365), channel_id=1, source_target_pairs={{0,1},{1,0},{2,3},{3,2},{4,5},{5,4},{6,7},{7,6},{8,9},{9,8},{10,11... | collective-permute-start | bytes 1769480 | tf_op jit(solution)/shard_map/ppermute | solution.py:971
  136.8 23.2 %collective-permute-start.16 = (bf16[96,3072]{1,0:T(8,128)(2,1)S(1)}, bf16[96,3072]{1,0:T(8,128)(2,1)S(1)}, u32[]{:S(2)}, u32[]{:S(2)}) collective-permute-start(bf16[96,3072]{1,0:T(8,128)(2,1)S(1)} %get-tuple-element.345), channel_id=1, source_target_pairs={{0,8},{1,5},{2,10},{3,7},{4,12},{5,1},{6,14},{7,3},{8,0},{9,13},{1... | collective-permute-start | bytes 1769480 | tf_op jit(solution)/shard_map/ppermute | solution.py:977
  143.6 27.2 %collective-permute-start.24 = (bf16[48,3072]{1,0:T(8,128)(2,1)S(1)}, bf16[48,3072]{1,0:T(8,128)(2,1)S(1)}, u32[]{:S(2)}, u32[]{:S(2)}) collective-permute-start(bf16[48,3072]{1,0:T(8,128)(2,1)S(1)} %add.83.mine_ref), channel_id=1, source_target_pairs={{0,2},{1,9},{2,0},{3,11},{4,6},{5,13},{6,4},{7,15},{8,10},{9,1},{1... | collective-permute-start | bytes 884744 | tf_op jit(solution)/shard_map/ppermute | solution.py:977
  144.9 25.9 %collective-permute-start.25 = (f32[16,768]{1,0:T(8,128)S(1)}, f32[16,768]{1,0:T(8,128)S(1)}, u32[]{:S(2)}, u32[]{:S(2)}) collective-permute-start(f32[16,768]{1,0:T(8,128)S(1)} %pack_vectors.1.mine_ref), channel_id=1, source_target_pairs={{0,1},{1,0},{2,3},{3,2},{4,5},{5,4},{6,7},{7,6},{8,9},{9,8},{10,11... | collective-permute-start | bytes 147464 | tf_op jit(solution)/shard_map/ppermute | solution.py:971
  146.2 31.9 %collective-permute-start.22 = (bf16[192,3072]{1,0:T(8,128)(2,1)S(1)}, bf16[192,3072]{1,0:T(8,128)(2,1)S(1)}, u32[]{:S(2)}, u32[]{:S(2)}) collective-permute-start(bf16[192,3072]{1,0:T(8,128)(2,1)S(1)} %get-tuple-element.374), channel_id=1, source_target_pairs={{0,4},{1,3},{2,6},{3,1},{4,0},{5,7},{6,2},{7,5},{8,12},{9,11},{10,... | collective-permute-start | bytes 3538952 | tf_op jit(solution)/shard_map/ppermute | solution.py:977
  160.7 10.7 %collective-permute-start.23 = (bf16[48,3072]{1,0:T(8,128)(2,1)S(1)}, bf16[48,3072]{1,0:T(8,128)(2,1)S(1)}, u32[]{:S(2)}, u32[]{:S(2)}) collective-permute-start(bf16[48,3072]{1,0:T(8,128)(2,1)S(1)} %get-tuple-element.377), channel_id=1, source_target_pairs={{0,2},{1,9},{2,0},{3,11},{4,6},{5,13},{6,4},{7,15},{8,10},{9,1},{1... | collective-permute-start | bytes 884744 | tf_op jit(solution)/shard_map/ppermute | solution.py:977
  171.4 17.2 %collective-permute-start.27 = (bf16[96,3072]{1,0:T(8,128)(2,1)S(1)}, bf16[96,3072]{1,0:T(8,128)(2,1)S(1)}, u32[]{:S(2)}, u32[]{:S(2)}) collective-permute-start(bf16[96,3072]{1,0:T(8,128)(2,1)S(1)} %join.9.mine_ref), channel_id=1, source_target_pairs={{0,8},{1,5},{2,10},{3,7},{4,12},{5,1},{6,14},{7,3},{8,0},{9,13},{1... | collective-permute-start | bytes 1769480 | tf_op jit(solution)/shard_map/ppermute | solution.py:977
  179.0 33.6 %collective-permute-start.26 = (bf16[96,3072]{1,0:T(8,128)(2,1)S(1)}, bf16[96,3072]{1,0:T(8,128)(2,1)S(1)}, u32[]{:S(2)}, u32[]{:S(2)}) collective-permute-start(bf16[96,3072]{1,0:T(8,128)(2,1)S(1)} %get-tuple-element.391), channel_id=1, source_target_pairs={{0,8},{1,5},{2,10},{3,7},{4,12},{5,1},{6,14},{7,3},{8,0},{9,13},{1... | collective-permute-start | bytes 1769480 | tf_op jit(solution)/shard_map/ppermute | solution.py:977
  189.2 31.7 %collective-permute-start.31 = (bf16[192,3072]{1,0:T(8,128)(2,1)S(1)}, bf16[192,3072]{1,0:T(8,128)(2,1)S(1)}, u32[]{:S(2)}, u32[]{:S(2)}) collective-permute-start(bf16[192,3072]{1,0:T(8,128)(2,1)S(1)} %join.10.mine_ref), channel_id=1, source_target_pairs={{0,4},{1,3},{2,6},{3,1},{4,0},{5,7},{6,2},{7,5},{8,12},{9,11},{10,... | collective-permute-start | bytes 3538952 | tf_op jit(solution)/shard_map/ppermute | solution.py:977
  189.3 24.8 %collective-permute-start.29 = (bf16[48,3072]{1,0:T(8,128)(2,1)S(1)}, bf16[48,3072]{1,0:T(8,128)(2,1)S(1)}, u32[]{:S(2)}, u32[]{:S(2)}) collective-permute-start(bf16[48,3072]{1,0:T(8,128)(2,1)S(1)} %add.85.mine_ref), channel_id=1, source_target_pairs={{0,2},{1,9},{2,0},{3,11},{4,6},{5,13},{6,4},{7,15},{8,10},{9,1},{1... | collective-permute-start | bytes 884744 | tf_op jit(solution)/shard_map/ppermute | solution.py:977
  213.4 6.8 %collective-permute-start.28 = (bf16[48,3072]{1,0:T(8,128)(2,1)S(1)}, bf16[48,3072]{1,0:T(8,128)(2,1)S(1)}, u32[]{:S(2)}, u32[]{:S(2)}) collective-permute-start(bf16[48,3072]{1,0:T(8,128)(2,1)S(1)} %get-tuple-element.397), channel_id=1, source_target_pairs={{0,2},{1,9},{2,0},{3,11},{4,6},{5,13},{6,4},{7,15},{8,10},{9,1},{1... | collective-permute-start | bytes 884744 | tf_op jit(solution)/shard_map/ppermute | solution.py:977
  220.2 6.8 %collective-permute-start.30 = (bf16[48,3072]{1,0:T(8,128)(2,1)S(1)}, bf16[48,3072]{1,0:T(8,128)(2,1)S(1)}, u32[]{:S(2)}, u32[]{:S(2)}) collective-permute-start(bf16[48,3072]{1,0:T(8,128)(2,1)S(1)} %add.86.mine_ref), channel_id=1, source_target_pairs={{0,2},{1,9},{2,0},{3,11},{4,6},{5,13},{6,4},{7,15},{8,10},{9,1},{1... | collective-permute-start | bytes 884744 | tf_op jit(solution)/shard_map/ppermute | solution.py:977
  220.9 20.7 %collective-permute-start.34 = (bf16[96,3072]{1,0:T(8,128)(2,1)S(1)}, bf16[96,3072]{1,0:T(8,128)(2,1)S(1)}, u32[]{:S(2)}, u32[]{:S(2)}) collective-permute-start(bf16[96,3072]{1,0:T(8,128)(2,1)S(1)} %join.11.mine_ref), channel_id=1, source_target_pairs={{0,8},{1,5},{2,10},{3,7},{4,12},{5,1},{6,14},{7,3},{8,0},{9,13},{1... | collective-permute-start | bytes 1769480 | tf_op jit(solution)/shard_map/ppermute | solution.py:977
  221.6 31.7 %collective-permute-start.38 = (bf16[384,3072]{1,0:T(8,128)(2,1)S(1)}, bf16[384,3072]{1,0:T(8,128)(2,1)S(1)}, u32[]{:S(2)}, u32[]{:S(2)}) collective-permute-start(bf16[384,3072]{1,0:T(8,128)(2,1)S(1)} %join.12.value_ref), channel_id=1, source_target_pairs={{0,1},{1,0},{2,3},{3,2},{4,5},{5,4},{6,7},{7,6},{8,9},{9,8},{10,11... | collective-permute-start | bytes 7077896 | tf_op jit(solution)/shard_map/ppermute | solution.py:971
  227.6 23.0 %collective-permute-start.32 = (bf16[96,3072]{1,0:T(8,128)(2,1)S(1)}, bf16[96,3072]{1,0:T(8,128)(2,1)S(1)}, u32[]{:S(2)}, u32[]{:S(2)}) collective-permute-start(bf16[96,3072]{1,0:T(8,128)(2,1)S(1)} %join.13.mine_ref), channel_id=1, source_target_pairs={{0,8},{1,5},{2,10},{3,7},{4,12},{5,1},{6,14},{7,3},{8,0},{9,13},{1... | collective-permute-start | bytes 1769480 | tf_op jit(solution)/shard_map/ppermute | solution.py:977
  228.6 13.7 %collective-permute-start.33 = (f32[16,768]{1,0:T(8,128)S(1)}, f32[16,768]{1,0:T(8,128)S(1)}, u32[]{:S(2)}, u32[]{:S(2)}) collective-permute-start(f32[16,768]{1,0:T(8,128)S(1)} %add.84.mine_ref), channel_id=1, source_target_pairs={{0,2},{1,3},{2,0},{3,1},{4,6},{5,7},{6,4},{7,5},{8,10},{9,11},{10,... | collective-permute-start | bytes 147464 | tf_op jit(solution)/shard_map/ppermute | solution.py:971
  242.2 21.5 %collective-permute-start.37 = (bf16[192,3072]{1,0:T(8,128)(2,1)S(1)}, bf16[192,3072]{1,0:T(8,128)(2,1)S(1)}, u32[]{:S(2)}, u32[]{:S(2)}) collective-permute-start(bf16[192,3072]{1,0:T(8,128)(2,1)S(1)} %join.14.mine_ref), channel_id=1, source_target_pairs={{0,4},{1,3},{2,6},{3,1},{4,0},{5,7},{6,2},{7,5},{8,12},{9,11},{10,... | collective-permute-start | bytes 3538952 | tf_op jit(solution)/shard_map/ppermute | solution.py:977
  251.3 25.6 %collective-permute-start.35 = (bf16[192,3072]{1,0:T(8,128)(2,1)S(1)}, bf16[192,3072]{1,0:T(8,128)(2,1)S(1)}, u32[]{:S(2)}, u32[]{:S(2)}) collective-permute-start(bf16[192,3072]{1,0:T(8,128)(2,1)S(1)} %join.15.mine_ref), channel_id=1, source_target_pairs={{0,4},{1,3},{2,6},{3,1},{4,0},{5,7},{6,2},{7,5},{8,12},{9,11},{10,... | collective-permute-start | bytes 3538952 | tf_op jit(solution)/shard_map/ppermute | solution.py:977
  251.4 25.5 %collective-permute-start.36 = (f32[16,768]{1,0:T(8,128)S(1)}, f32[16,768]{1,0:T(8,128)S(1)}, u32[]{:S(2)}, u32[]{:S(2)}) collective-permute-start(f32[16,768]{1,0:T(8,128)S(1)} %add.87.mine_ref), channel_id=1, source_target_pairs={{0,4},{1,5},{2,6},{3,7},{4,0},{5,1},{6,2},{7,3},{8,12},{9,13},{10,... | collective-permute-start | bytes 147464 | tf_op jit(solution)/shard_map/ppermute | solution.py:971
  264.4 16.2 %collective-permute-start.40 = (bf16[384,3072]{1,0:T(8,128)(2,1)S(1)}, bf16[384,3072]{1,0:T(8,128)(2,1)S(1)}, u32[]{:S(2)}, u32[]{:S(2)}) collective-permute-start(bf16[384,3072]{1,0:T(8,128)(2,1)S(1)} %join.16.value_ref), channel_id=1, source_target_pairs={{0,1},{1,0},{2,3},{3,2},{4,5},{5,4},{6,7},{7,6},{8,9},{9,8},{10,11... | collective-permute-start | bytes 7077896 | tf_op jit(solution)/shard_map/ppermute | solution.py:971
  277.7 8.7 %collective-permute-start.41 = (f32[16,768]{1,0:T(8,128)S(1)}, f32[16,768]{1,0:T(8,128)S(1)}, u32[]{:S(2)}, u32[]{:S(2)}) collective-permute-start(f32[16,768]{1,0:T(8,128)S(1)} %add.88.mine_ref), channel_id=1, source_target_pairs={{0,8},{1,9},{2,10},{3,11},{4,12},{5,13},{6,14},{7,15},{8,0},{9,1},... | collective-permute-start | bytes 147464 | tf_op jit(solution)/shard_map/ppermute | solution.py:971
  (20 other events, 131.8 us)
